TPU v7x, 32 devices: a whole 2x2x4 slice. The times are simulated.
32 devices in a mesh: sub: 16 (over z, y, x), node: 2 (over core).
Axes of the slice: x: 2, y: 2, z: 4, core: 2. Of those that a mesh axis runs over, the one named last changes fastest.
Arguments:
- search_vectors: float32 [16384, 256], P('sub'), may hold values from -60 to 60
- ritz_values: float32 [256], replicated, may hold values from -0.9 to 0.9
- matrix_blocks: float32 [128, 4, 128, 128], P('sub'), may hold values from -0.25 to 0.25
- block_lists: int32 [128, 4], P('sub'), may hold values from 0 to 127, as said below
- inverses: float32 [4, 2, 128, 128, 128], P('node', None, 'sub'), may hold values from -0.5 to 0.5
- panels: float32 [16, 512, 1024], P('sub'), may hold values from -0.1875 to 0.1875
- separator_map: int32 [16, 4], P('sub'), may hold values from 0 to 7, as said below
- separator_shift: float32 [1024], replicated, may hold values from -0.9 to 0.9
Outputs:
- normalized_vectors: float32 [16384, 256], P('sub', 'node')
Inputs may be any that keep to these rules, and one draw needn't show every extreme that they name: `block_lists`: entry 0 of row g is g; the other entries of row g are distinct blocks from g - 4 to g + 4, none equal to g. `separator_map`: the entries of one row are distinct.
All inputs are finite; a program needn't handle non-finite values.
Results may differ from a plain program's by a relative error of at most 0.0001.
Values sent between devices are 32-bit elements; how exact they have to be, the bound alone decides.
A program may use at most 64 MiB of HBM per device.

v0:
```python
import math

import jax
import jax.numpy as jnp
from jax import lax
from jax.sharding import PartitionSpec as P

HALO_BLOCKS = 4
SEP_GROUPS = 8


HIGHEST = lax.Precision.HIGHEST


def with_halo(shard, sides, width):
    for axis, dim in sides:
        size, length = (lax.axis_size(axis), shard.shape[dim])
        up = [(i, (i + 1) % size) for i in range(size - 1)]
        down = [(j, i) for i, j in up]
        last = lax.slice_in_dim(shard, length - width, length, axis=dim)
        first = lax.slice_in_dim(shard, 0, width, axis=dim)
        before = lax.ppermute(last, axis, up)
        after = lax.ppermute(first, axis, down)
        shard = jnp.concatenate([before, shard, after], axis=dim)
    return shard


def scale_coarse(summed, shift_rows, real_shift, imag_shift):
    real_gap = real_shift[:, None, None] - shift_rows[None, :, None]
    imag_gap = imag_shift[:, None, None]
    modulus = real_gap * real_gap + imag_gap * imag_gap
    real_part = summed[:, 0]
    imag_part = summed[:, 1]
    return jnp.stack(
        [
            (real_part * real_gap + imag_part * imag_gap) / modulus,
            (imag_part * real_gap - real_part * imag_gap) / modulus,
        ],
        axis=1,
    )


def shards(
    search_vectors,
    ritz_values,
    matrix_blocks,
    block_lists,
    inverses,
    panels,
    separator_map,
    separator_shift,
):
    row_count, width = search_vectors.shape
    block_count, degree_count, block_size, _ = matrix_blocks.shape
    node_count = lax.axis_size("node")
    col_count = width // node_count
    node_index = lax.axis_index("node")
    sub_index = lax.axis_index("sub")
    column_start = node_index * col_count
    local_index = block_lists - sub_index * block_count + HALO_BLOCKS
    own_columns = lax.dynamic_slice_in_dim(search_vectors, column_start, col_count, 1)
    own_ritz = lax.dynamic_slice_in_dim(ritz_values, column_start, col_count, 0)
    padded = with_halo(own_columns, (("sub", 0),), HALO_BLOCKS * block_size)
    picked = padded.reshape(block_count + 2 * HALO_BLOCKS, block_size, -1)[local_index]
    local_part = (
        jnp.einsum("bkij,bkjm->bim", matrix_blocks, picked, precision=HIGHEST).reshape(
            row_count, -1
        )
        - own_columns * own_ritz[None, :]
    )
    residual = lax.all_gather(local_part, "node", axis=1, tiled=True)
    node_local = inverses.shape[0]
    total_nodes = node_local * node_count
    node_ids = (node_index * node_local + jnp.arange(node_local, dtype=jnp.int32)).astype(
        jnp.float32
    )
    angles = math.pi * (node_ids + 0.5) / total_nodes
    real_shift = jnp.cos(angles)
    imag_shift = jnp.sin(angles)
    res_blocks = residual.reshape(block_count, block_size, width)
    first_guess = jnp.einsum("ncbij,bjm->ncbim", inverses, res_blocks, precision=HIGHEST).reshape(
        node_local, 2, row_count, width
    )
    my_panel = panels[0]
    sep_count = my_panel.shape[0] // block_size
    partial_value = jnp.einsum("sr,ncrm->ncsm", my_panel, first_guess, precision=HIGHEST)
    one_hot = (
        separator_map[0][:, None] == jnp.arange(SEP_GROUPS, dtype=jnp.int32)[None, :]
    ).astype(jnp.float32)
    spread = jnp.einsum(
        "pg,ncpkm->ncgkm",
        one_hot,
        partial_value.reshape(node_local, 2, sep_count, block_size, width),
        precision=HIGHEST,
    ).reshape(node_local, 2, SEP_GROUPS * block_size, width)
    summed_all = lax.psum(spread, "sub")
    scaled = scale_coarse(summed_all, separator_shift, real_shift, imag_shift)
    picked_back = jnp.einsum(
        "pg,ncgkm->ncpkm",
        one_hot,
        scaled.reshape(node_local, 2, SEP_GROUPS, block_size, width),
        precision=HIGHEST,
    ).reshape(node_local, 2, sep_count * block_size, width)
    spread_back = jnp.einsum("sr,ncsm->ncrm", my_panel, picked_back, precision=HIGHEST).reshape(
        node_local, 2, block_count, block_size, width
    )
    products = jnp.einsum("ncbij,ndbjm->ncdbim", inverses, spread_back, precision=HIGHEST).reshape(
        node_local, 2, 2, row_count, width
    )
    sol_real = first_guess[:, 0] - (products[:, 0, 0] - products[:, 1, 1])
    sol_imag = first_guess[:, 1] - (products[:, 0, 1] + products[:, 1, 0])
    weight_real = 2.0 / total_nodes * real_shift
    weight_imag = 2.0 / total_nodes * imag_shift
    weighted = jnp.sum(
        weight_real[:, None, None] * sol_real - weight_imag[:, None, None] * sol_imag, axis=0
    )
    node_total = lax.psum_scatter(weighted, "node", scatter_dimension=1, tiled=True)
    updated = lax.dynamic_slice_in_dim(search_vectors, column_start, col_count, 1) - node_total
    squares = lax.psum(jnp.sum(updated * updated, axis=0), "sub")
    total_rows = row_count * lax.axis_size("sub")
    return updated * lax.rsqrt(squares / total_rows + 1e-06)[None, :]


def solution(mesh):
    return jax.shard_map(
        shards,
        mesh=mesh,
        in_specs=(
            P("sub", None),
            P(),
            P("sub", None, None, None),
            P("sub", None),
            P("node", None, "sub", None, None),
            P("sub", None, None),
            P("sub", None),
            P(),
        ),
        out_specs=P("sub", "node"),
        check_vma=False,
    )
```

profile of v0, /device:TPU:0, one launch (start us, length us, event | category | flops | bytes accessed | tf_op | source)
XLA Modules:
  0.0 344.5 jit_solution(13921328892674392484)
XLA Ops:
  6.5 0.0 copy-start
  6.5 0.0 all-gather.2.cloned.1.call-start
  6.5 1.2 fusion.40
  7.8 4.9 %collective-permute-start = (f32[512,128]{1,0:T(8,128)S(1)}, f32[512,128]{1,0:T(8,128)S(1)}, u32[]{:S(2)}, u32[]{:S(2)}) collective-permute-start(f32[512,128]{1,0:T(8,128)S(1)} %get-tuple-element.9), channel_id=1, source_target_pairs={{0,2},{2,4},{4,6},{6,8},{8,10},{10,12},{12,14},{14,16},{16,18},{18... | collective-permute-start | bytes 786440 | tf_op jit(solution)/shard_map/ppermute | solution.py:22
  12.7 1.3 collective-permute-start.1
  14.0 0.7 compare_select_fusion
  14.6 0.1 copy.15
  14.7 0.1 reshape.141
  14.8 0.8 dynamic_slice.8
  15.6 1.1 constant_dynamic-slice_fusion.1
  16.6 7.2 %collective-permute-done = f32[512,128]{1,0:T(8,128)S(1)} collective-permute-done((f32[512,128]{1,0:T(8,128)S(1)}, f32[512,128]{1,0:T(8,128)S(1)}, u32[]{:S(2)}, u32[]{:S(2)}) %collective-permute-start) | collective-permute-done | bytes 262176 | tf_op jit(solution)/shard_map/ppermute | solution.py:22
  23.8 2.0 collective-permute-done.1
  25.9 1.0 pad_maximum_fusion
  26.9 2.0 gather_fusion
  28.9 0.0 copy-start.5
  28.9 4.7 %fusion.41 = f32[8,128,128,1]{1,2,3,0:T(8,128)S(1)} fusion(f32[8,4,128,128]{3,2,1,0:T(8,128)} %bitcast.141, f32[8,4,128,128]{3,2,1,0:T(8,128)} %param.10), kind=kOutput, calls=%fused_computation.59 | convolution fusion | flops 805306368 | bytes 4718592 | tf_op jit(solution)/shard_map/bkij,bkjm->bim/dot_general | solution.py:66
  33.6 0.0 copy-done.5
  33.6 0.9 bitcast_subtract_fusion
  34.5 0.0 all-gather.2.cloned.1.call-update
  34.5 0.3 all-reduce.2.cloned.1.call-start
  34.8 8.9 %all-gather.2.cloned.1.call-done = f32[1024,256]{1,0:T(8,128)} async-done(((f32[1024,128]{1,0:T(8,128)}), f32[1024,256]{1,0:T(8,128)}) %all-gather.2.cloned.1.call-update) | async-done | bytes 1048592 | tf_op jit(solution)/shard_map/all_gather | solution.py:71
  43.7 0.0 copy-done
  43.7 4.7 %convolution_bitcast_fusion.1 = f32[2,2,8,128,256]{4,3,1,0,2:T(8,128)S(1)} fusion(f32[8,128,256,1,1]{2,1,4,3,0:T(8,128)} %bitcast.145, f32[2,2,8,128,128]{4,3,2,1,0:T(8,128)S(1)} %copy-done), kind=kOutput, calls=%fused_computation.9 | convolution fusion | flops 1610612736 | bytes 7340032 | tf_op jit(solution)/shard_map/ncbij,bjm->ncbim/dot_general | solution.py:81
  48.5 0.0 copy-start.3
  48.5 0.4 copy.17
  48.9 0.0 copy-start.1
  48.9 2.0 copy-done.1
  50.9 0.0 copy-done.3
  50.9 15.0 %fusion.25 = f32[2,2,512,256]{2,3,1,0:T(8,128)} fusion(f32[2,2,1024,256]{3,2,1,0:T(8,128)S(1)} %bitcast.134, f32[1,512,1024]{2,1,0:T(8,128)S(1)} %copy-done.3), kind=kOutput, calls=%fused_computation.34 | convolution fusion | flops 6442450944 | bytes 8388608 | tf_op jit(solution)/shard_map/sr,ncrm->ncsm/dot_general | solution.py:86
  65.9 2.9 reshape.134
  68.8 0.0 copy-start.7
  68.8 4.1 %copy.20 = f32[2,2,4,128,256]{4,2,3,1,0:T(4,128)} copy(f32[2,2,4,128,256]{3,2,4,1,0:T(4,128)} %reshape.134) | data formatting | bytes 4194304 | tf_op jit(solution)/shard_map/reshape | solution.py:93
  72.9 0.0 copy-done.7
  72.9 3.8 %convolution_bitcast_fusion = f32[2,2,8,128,256]{4,2,3,1,0:T(8,128)S(1)} fusion(f32[2,2,4,128,256]{4,2,3,1,0:T(4,128)} %copy.20, s32[4]{0:T(128)S(1)} %bitcast.146), kind=kOutput, calls=%fused_computation.8 | convolution fusion | flops 50331680 | bytes 6291472 | tf_op jit(solution)/shard_map/pg,ncpkm->ncgkm/dot_general | solution.py:90
  76.7 3.3 copy.21
  80.0 0.0 copy-start.6
  80.0 0.0 all-reduce.2.cloned.1.call-update
  80.0 0.0 reduce-scatter.2.cloned.1.call-start
  80.2 0.5 copy-done.6
  80.7 0.1 broadcast_subtract_fusion
  80.8 168.9 %all-reduce.2.cloned.1.call-done = f32[2,2,1024,256]{3,2,1,0:T(8,128)} async-done(((f32[2,2,1024,256]{3,2,1,0:T(8,128)}), f32[2,2,1024,256]{3,2,1,0:T(8,128)}) %all-reduce.2.cloned.1.call-update) | async-done | bytes 4194320 | tf_op jit(solution)/shard_map/psum | solution.py:96
  249.7 2.7 add_divide_fusion
  252.4 1.2 copy.22
  253.7 1.2 copy.23
  254.9 2.1 fusion.28
  257.0 0.0 copy-start.4
  257.0 0.4 copy.24
  257.4 1.2 copy-done.4
  258.6 7.0 %fusion.19 = f32[2,2,256,1024]{3,2,1,0:T(8,128)S(1)} fusion(f32[2,2,512,256]{3,2,1,0:T(8,128)S(1)} %bitcast.144, f32[1,512,1024]{2,1,0:T(8,128)S(1)} %copy-done.4), kind=kOutput, calls=%fused_computation.26 | convolution fusion | flops 6442450944 | bytes 8388608 | tf_op jit(solution)/shard_map/sr,ncsm->ncrm/dot_general | solution.py:104
  265.6 1.2 copy.50
  266.8 7.8 %fusion.6 = f32[2,2,2,8,128,256]{5,4,1,2,3,0:T(8,128)S(1)} fusion(f32[2,2,8,128,256,1]{3,2,4,1,0,5:T(8,128)S(1)} %bitcast.137, f32[2,2,8,128,128]{4,3,2,1,0:T(8,128)S(1)} %copy-done), kind=kOutput, calls=%fused_computation.7 | convolution fusion | flops 3221225472 | bytes 14680064 | tf_op jit(solution)/shard_map/ncbij,ndbjm->ncdbim/dot_general | solution.py:107
  274.6 0.0 copy-start.2
  274.6 4.2 %copy.28 = f32[2,2,2,8,128,256]{5,4,3,2,1,0:T(8,128)} copy(f32[2,2,2,8,128,256]{5,4,1,2,3,0:T(8,128)S(1)} %fusion.6) | data formatting | bytes 16777216 | tf_op jit(solution)/shard_map/ncbij,ndbjm->ncdbim/transpose | solution.py:107
  278.8 0.0 copy-done.2
  278.8 5.6 %fusion.14 = f32[1024,256]{1,0:T(8,128)} fusion(f32[2,2,2,1024,256]{4,3,2,1,0:T(8,128)} %bitcast.136, f32[2,2,1024,256]{3,2,1,0:T(8,128)S(1)} %bitcast.135, f32[2]{0:T(128)S(1)} %get-tuple-element.13, f32[2]{0:T(128)S(1)} %get-tuple-element.14), kind=kLoop, calls=%fused_computation.16 | loop fusion | flops 3932160 | bytes 13631504 | tf_op jit(solution)/shard_map/reduce_sum | solution.py:114
  284.4 0.0 reduce-scatter.2.cloned.1.call-update
  284.4 7.6 %reduce-scatter.2.cloned.1.call-done = f32[1024,128]{1,0:T(8,128)} async-done(((f32[1024,256]{1,0:T(8,128)}), f32[1024,128]{1,0:T(8,128)}) %reduce-scatter.2.cloned.1.call-update) | async-done | bytes 524304 | tf_op jit(solution)/shard_map/reduce_scatter | solution.py:117
  292.0 1.9 multiply_reduce_fusion
  293.9 41.9 %psum.15 = f32[128]{0:T(128)S(1)} all-reduce(f32[128]{0:T(128)S(1)} %get-tuple-element.5), channel_id=1, replica_groups=mesh['sub'=16,'node'=2] {'sub'}, use_global_device_ids=true, to_apply=%region_4.0 | all-reduce | flops 128 | bytes 1024 | tf_op jit(solution)/shard_map/psum | solution.py:119
  335.8 1.9 broadcast_multiply_fusion
  (5 shorter events, 0.2 us)
Async XLA Ops:
  6.5 37.2 %copy-start = (f32[2,2,8,128,128]{4,3,2,1,0:T(8,128)S(1)}, f32[2,2,8,128,128]{4,3,2,1,0:T(8,128)}, u32[]{:S(2)}) copy-start(f32[2,2,8,128,128]{4,3,2,1,0:T(8,128)} %param.12) | copy-start | bytes 6291460
  6.5 37.2 %all-gather.2.cloned.1.call-start = ((), (), s32[]{:S(2)}) async-start(), calls=%async_computation.1 | async-start | bytes 1572864 | tf_op jit(solution)/shard_map/all_gather | solution.py:71
  7.8 16.1 %collective-permute-start = (f32[512,128]{1,0:T(8,128)S(1)}, f32[512,128]{1,0:T(8,128)S(1)}, u32[]{:S(2)}, u32[]{:S(2)}) collective-permute-start(f32[512,128]{1,0:T(8,128)S(1)} %get-tuple-element.9), channel_id=1, source_target_pairs={{0,2},{2,4},{4,6},{6,8},{8,10},{10,12},{12,14},{14,16},{16,18},{18... | collective-permute-start | bytes 786440 | tf_op jit(solution)/shard_map/ppermute | solution.py:22
  12.7 13.2 %collective-permute-start.1 = (f32[512,128]{1,0:T(8,128)S(1)}, f32[512,128]{1,0:T(8,128)}, u32[]{:S(2)}, u32[]{:S(2)}) collective-permute-start(f32[512,128]{1,0:T(8,128)S(1)} %get-tuple-element.10), channel_id=1, source_target_pairs={{2,0},{4,2},{6,4},{8,6},{10,8},{12,10},{14,12},{16,14},{18,16},{20... | collective-permute-start | bytes 786440 | tf_op jit(solution)/shard_map/ppermute | solution.py:23
  28.9 4.7 %copy-start.5 = (f32[1024,256]{1,0:T(8,128)S(1)}, f32[1024,256]{1,0:T(8,128)}, u32[]{:S(2)}) copy-start(f32[1024,256]{1,0:T(8,128)} %param.8) | copy-start | bytes 3145732
  34.5 215.2 %all-reduce.2.cloned.1.call-start = ((), (), s32[]{:S(2)}) async-start(), calls=%async_computation.2 | async-start | bytes 8388608 | tf_op jit(solution)/shard_map/psum | solution.py:96
  48.5 2.4 copy-start.3
  48.9 2.0 copy-start.1
  68.8 4.1 %copy-start.7 = (s32[1,4]{1,0:T(1,128)S(1)}, s32[1,4]{1,0:T(1,128)}, u32[]{:S(2)}) copy-start(s32[1,4]{1,0:T(1,128)} %param.14) | copy-start | bytes 52
  80.0 0.7 copy-start.6
  80.0 212.0 %reduce-scatter.2.cloned.1.call-start = ((), (), s32[]{:S(2)}) async-start(), calls=%async_computation.3 | async-start | bytes 1572864 | tf_op jit(solution)/shard_map/reduce_scatter | solution.py:117
  257.0 1.6 copy-start.4
  274.6 4.2 %copy-start.2 = (f32[2,2,8,128,256]{4,3,2,1,0:T(8,128)S(1)}, f32[2,2,8,128,256]{4,3,2,1,0:T(8,128)}, u32[]{:S(2)}) copy-start(f32[2,2,8,128,256]{4,3,2,1,0:T(8,128)} %copy-done.1) | copy-start | bytes 12582916
Sparse Core Ops, SparseCore 0:
  34.6 9.0 all-gather.1
  80.1 169.5 all-reduce.1
  284.5 7.4 reduce-scatter.1
where the time goes:
time: 348 us; the launch traced here: 344 us
  waiting for transfers between devices  195 us (56%)
  matrix products  45.1 us (13%)
  blocking collectives  41.9 us (12%)
  local copies, waits for them, and re-layouts  27.8 us (8%)
  other arithmetic  14.9 us (4%)
  between operations  13.5 us (4%)
  starting transfers between devices  6.56 us (2%)
    psum x1, waiting for transfers between devices, shards(): summed_all = lax.psum(spread, 'sub')  169 us
    psum x1, blocking collectives, shards(): squares = lax.psum(jnp.sum(updated * updated, axis=0), 'sub')  41.9 us
    dot_general x1, matrix products, shards(): jnp.einsum('sr,ncrm->ncsm', my_panel, first_guess, precision=HIGHEST)  15 us
    all_gather x1, waiting for transfers between devices, shards(): residual = lax.all_gather(local_part, 'node', axis=1, tiled=True)  8.89 us
    dot_general x1, matrix products, shards(): jnp.einsum('ncbij,ndbjm->ncdbim', inverses, spread_back, precision=HIGHEST)  7.8 us
    reduce_scatter x1, waiting for transfers between devices, shards(): lax.psum_scatter(weighted, 'node', scatter_dimension=1, tiled=True)  7.57 us
    ppermute x1, waiting for transfers between devices, with_halo(): before = lax.ppermute(last, axis, up)  7.18 us
    reshape x2, local copies, waits for them, and re-layouts, shards(): partial_value.reshape(node_local, 2, sep_count, block_size, width)  7.06 us
  transfers between devices with their start and end apart: 5, of which 5 were waited for; matrix products, arithmetic and copies ran while one was open for 1% of the time, Pallas kernels for 0%

commit v1 on v0

v1 whole, which is shorter than its diff:
```python
import functools
import math

import jax
import jax.numpy as jnp
from jax import lax
from jax.experimental import pallas as pl
from jax.experimental.pallas import tpu as pltpu
from jax.sharding import PartitionSpec as P

HALO_BLOCKS = 4
SEP_GROUPS = 8
HIGH = lax.Precision.HIGH
VMEM = pltpu.VMEM
SMEM = pltpu.SMEM


def split(x):
    hi = x.astype(jnp.bfloat16)
    lo = (x - hi.astype(jnp.float32)).astype(jnp.bfloat16)
    return hi, lo


def dot3(a, b):
    a_hi, a_lo = split(a)
    b_hi, b_lo = split(b)
    dot = functools.partial(jnp.dot, preferred_element_type=jnp.float32)
    return dot(a_hi, b_hi) + (dot(a_hi, b_lo) + dot(a_lo, b_hi))


def meet(targets):
    barrier = pltpu.get_barrier_semaphore()
    for target in targets:
        pl.semaphore_signal(
            barrier, inc=1, device_id=target, device_id_type=pl.DeviceIdType.MESH
        )
    pl.semaphore_wait(barrier, len(targets))


def remote(src, dst, send, recv, target):
    return pltpu.make_async_remote_copy(
        src_ref=src,
        dst_ref=dst,
        send_sem=send,
        recv_sem=recv,
        device_id=target,
        device_id_type=pl.DeviceIdType.MESH,
    )


def residual_kernel(
    subs, nodes, index_ref, own_ref, ritz_ref, blocks_ref, out_ref,
    padded, halo_send, halo_recv, own_sem, node_send, node_recv,
):
    sub, node = lax.axis_index("sub"), lax.axis_index("node")
    count = own_ref.shape[0]
    after, before = lax.rem(sub + 1, subs), lax.rem(sub + subs - 1, subs)
    others = [lax.rem(node + k, nodes) for k in range(1, nodes)]
    meet([{"sub": after}, {"sub": before}] + [{"node": o} for o in others])
    up = remote(
        own_ref.at[pl.ds(count - HALO_BLOCKS, HALO_BLOCKS)],
        padded.at[pl.ds(0, HALO_BLOCKS)],
        halo_send.at[0], halo_recv.at[0], {"sub": after},
    )
    down = remote(
        own_ref.at[pl.ds(0, HALO_BLOCKS)],
        padded.at[pl.ds(HALO_BLOCKS + count, HALO_BLOCKS)],
        halo_send.at[1], halo_recv.at[1], {"sub": before},
    )
    up.start()
    down.start()
    mine = pltpu.make_async_copy(own_ref, padded.at[pl.ds(HALO_BLOCKS, count)], own_sem)
    mine.start()
    mine.wait()
    up.wait()
    down.wait()

    def copies(b):
        return [
            remote(
                out_ref.at[node, b], out_ref.at[node, b],
                node_send.at[k, b], node_recv.at[k, b], {"node": o},
            )
            for k, o in enumerate(others)
        ]

    def step(b, carry):
        total = -(own_ref[b] * ritz_ref[...])
        for q in range(blocks_ref.shape[1]):
            total = total + dot3(blocks_ref[b, q], padded[index_ref[b, q]])
        out_ref[node, b] = total
        for copy in copies(b):
            copy.start()
        return carry

    lax.fori_loop(0, count, step, 0)

    def finish(b, carry):
        for copy in copies(b):
            copy.wait()
        return carry

    lax.fori_loop(0, count, finish, 0)


def residual_call(index, own, ritz, blocks, subs, nodes):
    count, size, width = own.shape
    return pl.pallas_call(
        functools.partial(residual_kernel, subs, nodes),
        out_shape=jax.ShapeDtypeStruct((nodes, count, size, width), jnp.float32),
        in_specs=[pl.BlockSpec(memory_space=SMEM)] + [pl.BlockSpec(memory_space=VMEM)] * 3,
        out_specs=pl.BlockSpec(memory_space=VMEM),
        scratch_shapes=[
            VMEM((count + 2 * HALO_BLOCKS, size, width), jnp.float32),
            pltpu.SemaphoreType.DMA((2,)),
            pltpu.SemaphoreType.DMA((2,)),
            pltpu.SemaphoreType.DMA,
            pltpu.SemaphoreType.DMA((nodes - 1, count)),
            pltpu.SemaphoreType.DMA((nodes - 1, count)),
        ],
        compiler_params=pltpu.CompilerParams(collective_id=0, has_side_effects=True),
        name="residual",
    )(index, own, ritz, blocks)


def separator_kernel(
    subs, cuts, map_ref, slot_ref, shift_ref, real_ref, imag_ref, part_ref, back_ref,
    landed, coarse, picked, send, recv, own_sem,
):
    sub = lax.axis_index("sub")
    node_local, _, panels, size, width = part_ref.shape
    rows, cols = size * cuts // subs, width // cuts
    others = [lax.rem(sub + k, subs) for k in range(1, subs)]
    meet([{"sub": o} for o in others])

    def piece(ref, owner):
        row = pl.multiple_of((owner // cuts) * rows, rows)
        col = pl.multiple_of(lax.rem(owner, cuts) * cols, cols) if cuts > 1 else 0
        return ref.at[:, :, :, pl.ds(row, rows), pl.ds(col, cols)]

    there = [
        remote(
            piece(part_ref, o), landed.at[sub, :, :, pl.ds(0, panels)],
            send.at[0, k], recv.at[0, k], {"sub": o},
        )
        for k, o in enumerate(others)
    ]
    for copy in there:
        copy.start()
    own = pltpu.make_async_copy(
        piece(part_ref, sub), landed.at[sub, :, :, pl.ds(0, panels)], own_sem.at[0]
    )
    own.start()
    landed[:, :, :, panels] = jnp.zeros((subs, node_local, 2, rows, cols), jnp.float32)
    own.wait()
    for copy in there:
        copy.wait()

    def group(g, carry):
        shift = shift_ref[g]
        for n in range(node_local):
            gap = real_ref[n] - shift
            imag = imag_ref[n]
            modulus = gap * gap + imag * imag
            by_real, by_imag = gap / modulus, imag / modulus

            def add(t, sums):
                slot = slot_ref[t, g]
                return (sums[0] + landed[t, n, 0, slot], sums[1] + landed[t, n, 1, slot])

            zero = jnp.zeros((rows, cols), jnp.float32)
            real, imaginary = lax.fori_loop(0, subs, add, (zero, zero))
            coarse[g, n, 0] = real * by_real + imaginary * by_imag
            coarse[g, n, 1] = imaginary * by_real - real * by_imag
        return carry

    lax.fori_loop(0, shift_ref.shape[0], group, 0)

    def pick(t, carry):
        for p in range(panels):
            value = coarse[map_ref[t, p]]
            for n in range(node_local):
                for c in range(2):
                    picked[t, n, c, p] = value[n, c]
        return carry

    lax.fori_loop(0, subs, pick, 0)
    home = [
        remote(
            picked.at[o], piece(back_ref, sub), send.at[1, k], recv.at[1, k], {"sub": o}
        )
        for k, o in enumerate(others)
    ]
    for copy in home:
        copy.start()
    own = pltpu.make_async_copy(picked.at[sub], piece(back_ref, sub), own_sem.at[1])
    own.start()
    own.wait()
    for copy in home:
        copy.wait()


def separator_call(maps, slots, shift, real_shift, imag_shift, part, subs):
    node_local, _, panels, size, width = part.shape
    cuts = max(1, subs * 8 // size)
    rows, cols = size * cuts // subs, width // cuts
    groups = shift.shape[0] // size
    row = (lax.axis_index("sub") // cuts) * rows
    my_shift = lax.dynamic_slice_in_dim(shift.reshape(groups, size, 1), row, rows, 1)
    my_shift = jnp.broadcast_to(my_shift, (groups, rows, cols))
    return pl.pallas_call(
        functools.partial(separator_kernel, subs, cuts),
        out_shape=jax.ShapeDtypeStruct(part.shape, jnp.float32),
        in_specs=[
            pl.BlockSpec(memory_space=SMEM),
            pl.BlockSpec(memory_space=SMEM),
            pl.BlockSpec(memory_space=VMEM),
            pl.BlockSpec(memory_space=SMEM),
            pl.BlockSpec(memory_space=SMEM),
            pl.BlockSpec(memory_space=VMEM),
        ],
        out_specs=pl.BlockSpec(memory_space=VMEM),
        scratch_shapes=[
            VMEM((subs, node_local, 2, panels + 1, rows, cols), jnp.float32),
            VMEM((groups, node_local, 2, rows, cols), jnp.float32),
            VMEM((subs, node_local, 2, panels, rows, cols), jnp.float32),
            pltpu.SemaphoreType.DMA((2, subs - 1)),
            pltpu.SemaphoreType.DMA((2, subs - 1)),
            pltpu.SemaphoreType.DMA((2,)),
        ],
        compiler_params=pltpu.CompilerParams(collective_id=1, has_side_effects=True),
        name="separator",
    )(maps, slots, my_shift, real_shift, imag_shift, part)


def update_kernel(
    subs, nodes, own_ref, weighted_ref, out_ref, landed, sums, node_send, node_recv, sub_send, sub_recv
):
    sub, node = lax.axis_index("sub"), lax.axis_index("node")
    others = [lax.rem(node + k, nodes) for k in range(1, nodes)]
    rest = [lax.rem(sub + k, subs) for k in range(1, subs)]
    meet([{"node": o} for o in others] + [{"sub": o} for o in rest])
    count = own_ref.shape[0]

    def copies(b):
        return [
            remote(
                weighted_ref.at[o, b], landed.at[k, b],
                node_send.at[k, b], node_recv.at[k, b], {"node": o},
            )
            for k, o in enumerate(others)
        ]

    def begin(b, carry):
        for copy in copies(b):
            copy.start()
        return carry

    lax.fori_loop(0, count, begin, 0)

    def step(b, squares):
        for copy in copies(b):
            copy.wait()
        total = own_ref[b] - weighted_ref[node, b]
        for k in range(nodes - 1):
            total = total - landed[k, b]
        out_ref[b] = total
        return squares + jnp.sum(total * total, axis=0, keepdims=True)

    width = own_ref.shape[2]
    squares = lax.fori_loop(0, count, step, jnp.zeros((1, width), jnp.float32))
    sums[sub] = jnp.broadcast_to(squares, (8, width))
    share = [
        remote(sums.at[sub], sums.at[sub], sub_send.at[k], sub_recv.at[k], {"sub": o})
        for k, o in enumerate(rest)
    ]
    for copy in share:
        copy.start()
    for copy in share:
        copy.wait()
    total = sums[0]
    for t in range(1, subs):
        total = total + sums[t]
    rows = count * own_ref.shape[1] * subs
    factor = lax.rsqrt(total / rows + 1e-06)[0:1]

    def scale(b, carry):
        out_ref[b] = out_ref[b] * factor
        return carry

    lax.fori_loop(0, count, scale, 0)


def update_call(own, weighted, subs, nodes):
    count, size, width = own.shape
    return pl.pallas_call(
        functools.partial(update_kernel, subs, nodes),
        out_shape=jax.ShapeDtypeStruct(own.shape, jnp.float32),
        in_specs=[pl.BlockSpec(memory_space=VMEM)] * 2,
        out_specs=pl.BlockSpec(memory_space=VMEM),
        scratch_shapes=[
            VMEM((nodes - 1, count, size, width), jnp.float32),
            VMEM((subs, 8, width), jnp.float32),
            pltpu.SemaphoreType.DMA((nodes - 1, count)),
            pltpu.SemaphoreType.DMA((nodes - 1, count)),
            pltpu.SemaphoreType.DMA((subs - 1,)),
            pltpu.SemaphoreType.DMA((subs - 1,)),
        ],
        compiler_params=pltpu.CompilerParams(collective_id=2, has_side_effects=True),
        name="update",
    )(own, weighted)


def shards(
    search_vectors,
    ritz_values,
    matrix_blocks,
    block_lists,
    inverses,
    panels,
    separator_map,
    separator_shift,
):
    row_count, width = search_vectors.shape
    block_count, _, block_size, _ = matrix_blocks.shape
    nodes, subs = lax.axis_size("node"), lax.axis_size("sub")
    col_count = width // nodes
    node_index = lax.axis_index("node")
    sub_index = lax.axis_index("sub")
    column_start = node_index * col_count
    maps = lax.all_gather(separator_map, "sub", axis=0, tiled=True)
    own_columns = lax.dynamic_slice_in_dim(search_vectors, column_start, col_count, 1)
    own_columns = own_columns.reshape(block_count, block_size, col_count)
    own_ritz = lax.dynamic_slice_in_dim(ritz_values, column_start, col_count, 0)[None, :]
    local_index = block_lists - sub_index * block_count + HALO_BLOCKS
    residual = residual_call(local_index, own_columns, own_ritz, matrix_blocks, subs, nodes)
    residual = residual.transpose(1, 2, 0, 3).reshape(block_count, block_size, width)

    node_local = inverses.shape[0]
    total_nodes = node_local * nodes
    node_ids = (node_index * node_local + jnp.arange(node_local, dtype=jnp.int32)).astype(
        jnp.float32
    )
    angles = math.pi * (node_ids + 0.5) / total_nodes
    real_shift = jnp.cos(angles)
    imag_shift = jnp.sin(angles)
    first_guess = jnp.einsum("ncbij,bjm->ncbim", inverses, residual, precision=HIGH).reshape(
        node_local, 2, row_count, width
    )
    my_panel = panels[0]
    sep_count = my_panel.shape[0] // block_size
    partial_value = jnp.einsum("sr,ncrm->ncsm", my_panel, first_guess, precision=HIGH)
    hits = maps[:, :, None] == jnp.arange(SEP_GROUPS, dtype=jnp.int32)[None, None, :]
    slots = sep_count - jnp.sum(
        hits * (sep_count - jnp.arange(sep_count, dtype=jnp.int32))[None, :, None], axis=1
    )
    picked_back = separator_call(
        maps, slots, separator_shift, real_shift, imag_shift,
        partial_value.reshape(node_local, 2, sep_count, block_size, width), subs,
    ).reshape(node_local, 2, sep_count * block_size, width)
    spread_back = jnp.einsum("sr,ncsm->ncrm", my_panel, picked_back, precision=HIGH).reshape(
        node_local, 2, block_count, block_size, width
    )
    weight_real = (2.0 / total_nodes * real_shift)[:, None, None, None]
    weight_imag = (2.0 / total_nodes * imag_shift)[:, None, None, None]
    by_real = weight_real * inverses[:, 0] - weight_imag * inverses[:, 1]
    by_imag = weight_real * inverses[:, 1] + weight_imag * inverses[:, 0]
    weighted = jnp.zeros((block_count, block_size, width), jnp.float32)
    for n in range(node_local):
        weighted = weighted + jnp.einsum(
            "bij,bjm->bim", by_real[n], residual - spread_back[n, 0], precision=HIGH
        )
        weighted = weighted + jnp.einsum(
            "bij,bjm->bim", by_imag[n], spread_back[n, 1], precision=HIGH
        )
    weighted = weighted.reshape(block_count, block_size, nodes, col_count).transpose(2, 0, 1, 3)
    return update_call(own_columns, weighted, subs, nodes).reshape(row_count, col_count)


def solution(mesh):
    return jax.shard_map(
        shards,
        mesh=mesh,
        in_specs=(
            P("sub", None),
            P(),
            P("sub", None, None, None),
            P("sub", None),
            P("node", None, "sub", None, None),
            P("sub", None, None),
            P("sub", None),
            P(),
        ),
        out_specs=P("sub", "node"),
        check_vma=False,
    )
```

time: 348 us -> 227 us (0.65)
  waiting for transfers between devices: 195 us -> 0 us
  Pallas kernels: 0 us -> 134 us
  matrix products: 45.1 us -> 25.6 us
  between operations: 13.5 us -> 0.13 us
  other arithmetic: 14.9 us -> 3.27 us
  starting transfers between devices: 6.56 us -> 0 us
    psum x1 -> x0, waiting for transfers between devices: 169 us -> none  [shards(): summed_all = lax.psum(spread, 'sub')]
    pallas_call x0 -> x3, Pallas kernels: none -> 134 us  [the longest x1 85.4 us: separator_call(): pl.pallas_call(functools.partial(separator_kernel, subs, cuts), out_shape...]
    psum x1 -> x0, blocking collectives: 41.9 us -> none  [shards(): squares = lax.psum(jnp.sum(updated * updated, axis=0), 'sub')]
    all_gather x0 -> x1, blocking collectives: none -> 38.9 us  [shards(): maps = lax.all_gather(separator_map, 'sub', axis=0, tiled=True)]
    dot_general x7, matrix products: 45.1 us -> 25.6 us  [the longest x1 7.99 us: shards(): jnp.einsum('sr,ncrm->ncsm', my_panel, first_guess, precision=HIGH)]
    ppermute x2 -> x0, waiting for transfers between devices: 9.2 us -> none  [the longest x1 7.18 us: with_halo(): before = lax.ppermute(last, axis, up)]
    all_gather x1 -> x0, waiting for transfers between devices: 8.89 us -> none  [shards(): residual = lax.all_gather(local_part, 'node', axis=1, tiled=True)]
    reduce_scatter x1 -> x0, waiting for transfers between devices: 7.57 us -> none  [shards(): lax.psum_scatter(weighted, 'node', scatter_dimension=1, tiled=True)]
  transfers between devices with their start and end apart: 5 -> 0, of which waited for: 5 -> 0; matrix products, arithmetic and copies ran while one was open for 1% -> 0% of each run, Pallas kernels for 0% -> 0%
where the time goes in v1:
time: 227 us
  Pallas kernels  134 us (59%)
  blocking collectives  38.9 us (17%)
  matrix products  25.6 us (11%)
  local copies, waits for them, and re-layouts  25.2 us (11%)
  other arithmetic  3.27 us (1%)
    pallas_call x1, Pallas kernels, separator_call(): pl.pallas_call(functools.partial(separator_kernel, subs, cuts), out_shape...  85.4 us
    all_gather x1, blocking collectives, shards(): maps = lax.all_gather(separator_map, 'sub', axis=0, tiled=True)  38.9 us
    pallas_call x1, Pallas kernels, update_call(): pl.pallas_call(functools.partial(update_kernel, subs, nodes), out_shape=j...  26.1 us
    pallas_call x1, Pallas kernels, residual_call(): pl.pallas_call(functools.partial(residual_kernel, subs, nodes), out_shape...  22.1 us
    unnamed x22, local copies, waits for them, and re-layouts  11.4 us
    dot_general x1, matrix products, shards(): jnp.einsum('sr,ncrm->ncsm', my_panel, first_guess, precision=HIGH)  7.99 us
    dot_general x2, matrix products, shards(): jnp.einsum('bij,bjm->bim', by_imag[n], spread_back[n, 1], precision=HIGH)  5.54 us
    dot_general x1, matrix products, shards(): jnp.einsum('sr,ncsm->ncrm', my_panel, picked_back, precision=HIGH)  5.11 us

profile of v1, /device:TPU:0, one launch (start us, length us, event | category | flops | bytes accessed | tf_op | source)
XLA Modules:
  0.0 226.6 jit_solution(4033457338015515992)
XLA Ops:
  0.0 0.0 copy-start
  0.0 2.0 constant_dynamic-slice_fusion
  2.0 1.3 dynamic-slice_bitcast_fusion.1.ritz_ref
  3.3 0.8 copy.87
  4.1 0.6 subtract_add_fusion.index_ref
  4.7 22.1 %residual.1 = f32[2,8,128,128]{3,2,1,0:T(8,128)} custom-call(s32[8,4]{1,0:T(8,128)} %subtract_add_fusion.index_ref, f32[8,128,128]{2,1,0:T(8,128)} %bitcast.100, f32[1,128]{1,0:T(1,128)} %dynamic-slice_bitcast_fusion.1.ritz_ref, f32[8,4,128,128]{3,2,1,0:T(8,128)} %blocks_ref.1), custom_call_target="tpu_custom_call" | custom-call | tf_op jit(solution)/shard_map/residual/pallas_call | solution.py:108
  26.7 1.6 copy.88
  28.3 3.4 %convolution_bitcast_fusion = f32[2,2,8,128,256]{4,3,1,0,2:T(8,128)S(1)} fusion(f32[8,128,256,1,1]{1,2,4,3,0:T(8,128)S(1)} %bitcast.92, f32[2,2,8,128,128]{4,3,2,1,0:T(8,128)} %param.12), kind=kOutput, calls=%fused_computation | convolution fusion | flops 805306368 | bytes 7340032 | tf_op jit(solution)/shard_map/ncbij,bjm->ncbim/dot_general | solution.py:347
  31.7 0.4 copy.94
  32.1 0.0 copy-done
  32.1 8.0 %fusion.5 = f32[2,2,512,256]{2,3,1,0:T(8,128)} fusion(f32[2,2,1024,256]{3,2,1,0:T(8,128)S(1)} %bitcast.96, f32[1,512,1024]{2,1,0:T(8,128)S(1)} %copy-done), kind=kOutput, calls=%fused_computation.6 | convolution fusion | flops 3221225472 | bytes 8388608 | tf_op jit(solution)/shard_map/sr,ncrm->ncsm/dot_general | solution.py:352
  40.1 0.0 copy-start.6
  40.1 0.0 copy-start.7
  40.1 3.0 %copy.96 = f32[2,2,512,256]{3,2,1,0:T(8,128)} copy(f32[2,2,512,256]{2,3,1,0:T(8,128)} %fusion.5) | data formatting | bytes 4194304 | tf_op jit(solution)/shard_map/sr,ncrm->ncsm/transpose | solution.py:352
  43.1 0.0 copy-done.6
  43.1 0.1 dynamic-slice_bitcast_fusion
  43.2 0.7 broadcast_in_dim.8.shift_ref
  43.9 0.6 fusion.17
  44.5 0.0 copy-done.7
  44.5 38.9 %all-gather = s32[16,1,4]{2,1,0:T(1,128)S(1)} all-gather(s32[1,1,4]{2,1,0:T(1,128)S(1)} %bitcast.109), channel_id=1, replica_groups=mesh['sub'=16,'node'=2] {'sub'}, dimensions={0}, use_global_device_ids=true | all-gather | bytes 272 | tf_op jit(solution)/shard_map/all_gather | solution.py:331
  83.4 0.1 copy.89
  83.5 0.1 select_reduce_fusion
  83.6 0.1 copy.91
  83.7 0.6 broadcast_subtract_fusion.slot_ref
  84.3 0.7 copy.97.map_ref
  84.9 85.4 %separator.1 = f32[2,2,4,128,256]{4,3,2,1,0:T(8,128)} custom-call(s32[16,4]{1,0:T(8,128)} %copy.97.map_ref, s32[16,8]{1,0:T(8,128)} %broadcast_subtract_fusion.slot_ref, f32[8,8,256]{2,1,0:T(8,128)} %broadcast_in_dim.8.shift_ref, f32[2]{0:T(128)} %get-tuple-element.14.real_ref, f32[2]{0:T(128)} %get-tuple-element.13.imag_ref, f32[2,2,4,128,256]{4,3,2,1,0:T(8,128)} %bitcast.98), custom_call_target="tpu_custom_call" | custom-call | tf_op jit(solution)/shard_map/separator/pallas_call | solution.py:211
  170.3 5.1 %fusion = f32[2,2,256,1024]{3,2,1,0:T(8,128)S(1)} fusion(f32[2,2,512,256]{3,2,1,0:T(8,128)} %bitcast.99, f32[1,512,1024]{2,1,0:T(8,128)S(1)} %copy-done), kind=kOutput, calls=%fused_computation.1 | convolution fusion | flops 3221225472 | bytes 8388608 | tf_op jit(solution)/shard_map/sr,ncsm->ncrm/dot_general | solution.py:361
  175.4 1.0 copy.121
  176.4 0.0 copy-start.1
  176.4 1.7 fusion.19
  178.2 0.9 copy-done.1
  179.2 1.3 fusion.9
  180.5 0.0 copy-start.3
  180.5 1.0 copy-done.3
  181.4 1.8 fusion.13
  183.2 2.6 %copy.118 = f32[1,1,8,128,256]{4,3,2,1,0:T(8,128)} copy(f32[1,1,8,128,256]{3,2,4,1,0:T(8,128)} %get-tuple-element.6) | data formatting | bytes 2097152
  185.8 0.0 copy-start.4
  185.8 0.0 copy-start.5
  185.8 2.4 %convolution_add_fusion.2 = f32[8,128,256]{2,1,0:T(8,128)S(1)} fusion(f32[8,128,256]{2,1,0:T(8,128)} %fusion.13, f32[1,1,8,128,256]{4,3,2,1,0:T(8,128)} %copy.118, f32[2,8,128,128]{3,2,1,0:T(8,128)} %get-tuple-element.9), kind=kOutput, calls=%fused_computation.9 | convolution fusion | flops 201588736 | bytes 3670016 | tf_op jit(solution)/shard_map/bij,bjm->bim/dot_general | solution.py:373
  188.2 0.0 copy-done.4
  188.2 0.0 copy-done.5
  188.2 1.8 convolution_add_fusion.1
  190.0 0.0 copy-start.2
  190.1 2.6 %copy.120 = f32[1,1,8,128,256]{4,3,2,1,0:T(8,128)} copy(f32[1,1,8,128,256]{3,2,4,1,0:T(8,128)} %get-tuple-element.5) | data formatting | bytes 2097152
  192.7 0.0 copy-done.2
  192.7 3.1 %convolution_add_fusion = f32[8,128,256]{2,1,0:T(8,128)} fusion(f32[8,128,256]{2,1,0:T(8,128)} %convolution_add_fusion.1, f32[1,1,8,128,256]{4,3,2,1,0:T(8,128)} %copy.120, f32[2,8,128,128]{3,2,1,0:T(8,128)S(1)} %copy-done.2), kind=kOutput, calls=%fused_computation.7 | convolution fusion | flops 201588736 | bytes 3670016 | tf_op jit(solution)/shard_map/bij,bjm->bim/dot_general | solution.py:373
  195.8 1.5 copy.105
  197.4 1.3 copy.106
  198.7 26.1 %update.1 = f32[8,128,128]{2,1,0:T(8,128)} custom-call(f32[8,128,128]{2,1,0:T(8,128)} %bitcast.101, f32[2,8,128,128]{3,2,1,0:T(8,128)} %bitcast.103), custom_call_target="tpu_custom_call" | custom-call | tf_op jit(solution)/shard_map/update/pallas_call | solution.py:296
  224.8 1.9 copy.133
  (2 shorter events, 0.0 us)
Async XLA Ops:
  0.0 32.1 %copy-start = (f32[1,512,1024]{2,1,0:T(8,128)S(1)}, f32[1,512,1024]{2,1,0:T(8,128)}, u32[]{:S(2)}) copy-start(f32[1,512,1024]{2,1,0:T(8,128)} %param.13) | copy-start | bytes 6291460
  40.1 3.0 %copy-start.6 = (f32[1024]{0:T(1024)S(1)}, f32[1024]{0:T(1024)}, u32[]{:S(2)}) copy-start(f32[1024]{0:T(1024)} %param.15) | copy-start | bytes 12292
  40.1 4.4 %copy-start.7 = (s32[1,4]{1,0:T(1,128)S(1)}, s32[1,4]{1,0:T(1,128)}, u32[]{:S(2)}) copy-start(s32[1,4]{1,0:T(1,128)} %param.14) | copy-start | bytes 52
  176.4 2.7 %copy-start.1 = (f32[2,2,8,128,128]{4,3,2,1,0:T(8,128)S(1)}, f32[2,2,8,128,128]{4,3,2,1,0:T(8,128)}, u32[]{:S(2)}) copy-start(f32[2,2,8,128,128]{4,3,2,1,0:T(8,128)} %param.12) | copy-start | bytes 6291460
  180.5 1.0 copy-start.3
  185.8 2.4 %copy-start.4 = (f32[2,8,128,128]{3,2,1,0:T(8,128)S(1)}, f32[2,8,128,128]{3,2,1,0:T(8,128)}, u32[]{:S(2)}) copy-start(f32[2,8,128,128]{3,2,1,0:T(8,128)} %copy-done.3) | copy-start | bytes 3145732
  185.8 2.4 %copy-start.5 = (f32[1,1,8,128,256]{3,2,4,1,0:T(8,128)S(1)}, f32[1,1,8,128,256]{3,2,4,1,0:T(8,128)}, u32[]{:S(2)}) copy-start(f32[1,1,8,128,256]{3,2,4,1,0:T(8,128)} %get-tuple-element.8) | copy-start | bytes 3145732
  190.0 2.6 %copy-start.2 = (f32[2,8,128,128]{3,2,1,0:T(8,128)S(1)}, f32[2,8,128,128]{3,2,1,0:T(8,128)}, u32[]{:S(2)}) copy-start(f32[2,8,128,128]{3,2,1,0:T(8,128)} %get-tuple-element.9) | copy-start | bytes 3145732

commit v2 on v0

v2 whole, which is shorter than its diff:
```python
import functools
import math

import jax
import jax.numpy as jnp
from jax import lax
from jax.experimental import pallas as pl
from jax.experimental.pallas import tpu as pltpu
from jax.sharding import PartitionSpec as P

HALO_BLOCKS = 4
SEP_GROUPS = 8
VMEM = pltpu.VMEM
SMEM = pltpu.SMEM


def split(x):
    hi = x.astype(jnp.bfloat16)
    lo = (x - hi.astype(jnp.float32)).astype(jnp.bfloat16)
    return hi, lo


def dot_halves(a, b):
    (a_hi, a_lo), (b_hi, b_lo) = a, b
    dot = functools.partial(jnp.dot, preferred_element_type=jnp.float32)
    return dot(a_hi, b_hi) + (dot(a_hi, b_lo) + dot(a_lo, b_hi))


def dot3(a, b):
    return dot_halves(split(a), split(b))


def meet(targets):
    barrier = pltpu.get_barrier_semaphore()
    for target in targets:
        pl.semaphore_signal(
            barrier, inc=1, device_id=target, device_id_type=pl.DeviceIdType.MESH
        )
    pl.semaphore_wait(barrier, len(targets))


def remote(src, dst, send, recv, target):
    return pltpu.make_async_remote_copy(
        src_ref=src,
        dst_ref=dst,
        send_sem=send,
        recv_sem=recv,
        device_id=target,
        device_id_type=pl.DeviceIdType.MESH,
    )


def inner_size(subs):
    return max(k for k in range(1, subs + 1) if subs % k == 0 and k * k <= subs)


def kernel(
    subs, nodes, inner, cuts, halves,
    index_ref, map_ref, own_ref, ritz_ref, shift_ref, blocks_hbm, inverses_hbm, panel_hbm,
    out_ref, squares_ref,
    blocks, inverses, panel, padded, maps, residual,
    panel_hi, panel_lo, turned_hi, turned_lo, fold_hi, fold_lo, guess_hi, guess_lo,
    part, near, dense, far, coarse, picked, back, weighted, shares, landed, sums,
    load_sem, halo_send, halo_recv, map_send, map_recv, node_send, node_recv,
    sep_send, sep_recv, far_send, far_recv, own_sem,
    share_send, share_recv, sum_send, sum_recv,
):
    sub, node = lax.axis_index("sub"), lax.axis_index("node")
    count, size, _ = own_ref.shape
    node_local = inverses.shape[0]
    total_nodes = node_local * nodes
    outer = subs // inner
    sep_blocks = map_ref.shape[0]
    groups, rows, cols = shift_ref.shape
    span = size // inner
    wide = part.shape[-1]
    width = wide * halves
    place, plane = lax.rem(sub, inner), sub // inner
    base = plane * inner
    near_places = [lax.rem(place + k, inner) for k in range(1, inner)]
    far_planes = [lax.rem(plane + k, outer) for k in range(1, outer)]
    other_nodes = [lax.rem(node + k, nodes) for k in range(1, nodes)]
    other_subs = [lax.rem(sub + k, subs) for k in range(1, subs)]
    after, before = lax.rem(sub + 1, subs), lax.rem(sub + subs - 1, subs)

    loads = [
        pltpu.make_async_copy(panel_hbm, panel, load_sem.at[0]),
        pltpu.make_async_copy(inverses_hbm, inverses, load_sem.at[1]),
        pltpu.make_async_copy(blocks_hbm, blocks, load_sem.at[2]),
        pltpu.make_async_copy(own_ref, padded.at[pl.ds(HALO_BLOCKS, count)], load_sem.at[3]),
        pltpu.make_async_copy(map_ref, maps.at[place], load_sem.at[4]),
    ]
    for load in loads:
        load.start()
    meet([{"sub": o} for o in other_subs] + [{"node": o} for o in other_nodes])
    halo = [
        remote(
            own_ref.at[pl.ds(count - HALO_BLOCKS, HALO_BLOCKS)],
            padded.at[pl.ds(0, HALO_BLOCKS)],
            halo_send.at[0], halo_recv.at[0], {"sub": after},
        ),
        remote(
            own_ref.at[pl.ds(0, HALO_BLOCKS)],
            padded.at[pl.ds(HALO_BLOCKS + count, HALO_BLOCKS)],
            halo_send.at[1], halo_recv.at[1], {"sub": before},
        ),
    ]
    tell = [
        remote(map_ref, maps.at[place], map_send.at[k], map_recv.at[k], {"sub": base + t})
        for k, t in enumerate(near_places)
    ]
    for copy in halo + tell:
        copy.start()

    def constant(values):
        chosen = jnp.float32(values[0])
        for k in range(1, nodes):
            chosen = jnp.where(node == k, jnp.float32(values[k]), chosen)
        return chosen

    angles = [
        [math.pi * (k * node_local + n + 0.5) / total_nodes for k in range(nodes)]
        for n in range(node_local)
    ]
    real_shift = [constant([math.cos(a) for a in row]) for row in angles]
    imag_shift = [constant([math.sin(a) for a in row]) for row in angles]
    real_weight = [constant([2.0 * math.cos(a) / total_nodes for a in row]) for row in angles]
    imag_weight = [constant([2.0 * math.sin(a) / total_nodes for a in row]) for row in angles]

    loads[0].wait()
    for p in range(sep_blocks):
        block = panel[p * size : (p + 1) * size]
        hi, lo = split(block)
        panel_hi[p * size : (p + 1) * size] = hi
        panel_lo[p * size : (p + 1) * size] = lo
        hi, lo = split(block.T)
        turned_hi[:, p * size : (p + 1) * size] = hi
        turned_lo[:, p * size : (p + 1) * size] = lo
    loads[1].wait()
    for n in range(node_local):

        def fold(b, carry):
            real, imag = inverses[n, 0, b], inverses[n, 1, b]
            hi, lo = split(real_weight[n] * real - imag_weight[n] * imag)
            fold_hi[n, b, :, :size], fold_lo[n, b, :, :size] = hi, lo
            hi, lo = split(real_weight[n] * imag + imag_weight[n] * real)
            fold_hi[n, b, :, size:], fold_lo[n, b, :, size:] = hi, lo
            return carry

        lax.fori_loop(0, count, fold, 0)
    for load in loads[2:]:
        load.wait()
    for copy in halo:
        copy.wait()

    def node_copies(b):
        return [
            remote(
                residual.at[node, b], residual.at[node, b],
                node_send.at[k, b], node_recv.at[k, b], {"node": o},
            )
            for k, o in enumerate(other_nodes)
        ]

    def residual_step(b, carry):
        total = -(own_ref[b] * ritz_ref[...])
        for q in range(blocks.shape[1]):
            total = total + dot3(blocks[b, q], padded[index_ref[b, q]])
        residual[node, b] = total
        for copy in node_copies(b):
            copy.start()
        return carry

    lax.fori_loop(0, count, residual_step, 0)

    def whole_residual(b):
        return jnp.concatenate([residual[j, b] for j in range(nodes)], axis=1)

    def guess_step(b, carry):
        for copy in node_copies(b):
            copy.wait()
        right = split(whole_residual(b))
        for n in range(node_local):
            for c in range(2):
                hi, lo = split(dot_halves(split(inverses[n, c, b]), right))
                for h in range(halves):
                    k = n * halves + h
                    chosen = slice(h * wide, (h + 1) * wide)
                    spot = slice(c * wide, (c + 1) * wide)
                    guess_hi[k, b, :, spot] = hi[:, chosen]
                    guess_lo[k, b, :, spot] = lo[:, chosen]
        return carry

    lax.fori_loop(0, count, guess_step, 0)
    for copy in tell:
        copy.wait()

    def strip(ref, t):
        return ref.at[:, :, pl.ds(pl.multiple_of(t * span, span), span)]

    def spot(ref, o):
        row = pl.multiple_of((o // cuts) * rows, rows)
        if cuts == 1:
            return ref.at[:, :, pl.ds(row, rows)]
        col = pl.multiple_of(lax.rem(o, cuts) * cols, cols)
        return ref.at[:, :, pl.ds(row, rows), pl.ds(col, cols)]

    def own_copy(k, src, dst, which):
        return pltpu.make_async_copy(src, dst, own_sem.at[k, which])

    def there_near(k):
        return [
            remote(
                strip(part.at[k], t), near.at[k, place],
                sep_send.at[k, 0, i], sep_recv.at[k, 0, i], {"sub": base + t},
            )
            for i, t in enumerate(near_places)
        ]

    def there_far(k):
        return [
            remote(
                spot(dense.at[k], z), far.at[k, plane],
                far_send.at[k, 0, i], far_recv.at[k, 0, i], {"sub": z * inner + place},
            )
            for i, z in enumerate(far_planes)
        ]

    def home_far(k):
        return [
            remote(
                spot(coarse.at[k], plane), spot(coarse.at[k], plane),
                far_send.at[k, 1, i], far_recv.at[k, 1, i], {"sub": z * inner + place},
            )
            for i, z in enumerate(far_planes)
        ]

    def home_near(k):
        return [
            remote(
                picked.at[k, t], strip(back.at[k], place),
                sep_send.at[k, 1, i], sep_recv.at[k, 1, i], {"sub": base + t},
            )
            for i, t in enumerate(near_places)
        ]

    def begin(copies):
        for copy in copies:
            copy.start()

    def finish(copies):
        for copy in copies:
            copy.wait()

    def stage_a(k):
        rights = (
            guess_hi[k].reshape(count * size, 2 * wide),
            guess_lo[k].reshape(count * size, 2 * wide),
        )
        value = dot_halves((panel_hi[...], panel_lo[...]), rights)
        value = value.reshape(sep_blocks, size, 2 * wide)
        part[k, 0] = value[:, :, :wide]
        part[k, 1] = value[:, :, wide:]
        begin(there_near(k))
        own_copy(k, strip(part.at[k], place), near.at[k, place], 0).start()

    def stage_b(k):
        finish(there_near(k))
        own_copy(k, strip(part.at[k], place), near.at[k, place], 0).wait()

        def group(g, carry):
            number = g.astype(jnp.float32)

            def add(t, totals):
                for p in range(sep_blocks):
                    hit = jnp.broadcast_to(maps[t, p, 0:1], (span, wide)) == number
                    totals = tuple(
                        total + jnp.where(hit, near[k, t, c, p], 0.0)
                        for c, total in enumerate(totals)
                    )
                return totals

            zero = jnp.zeros((span, wide), jnp.float32)
            totals = (zero, zero)
            for t in range(inner):
                totals = add(t, totals)
            dense[k, 0, g], dense[k, 1, g] = totals
            return carry

        lax.fori_loop(0, groups, group, 0)
        begin(there_far(k))
        own_copy(k, spot(dense.at[k], plane), far.at[k, plane], 1).start()

    def stage_c(k):
        finish(there_far(k))
        own_copy(k, spot(dense.at[k], plane), far.at[k, plane], 1).wait()
        n = k // halves
        gap = real_shift[n] - shift_ref[...]
        modulus = gap * gap + imag_shift[n] * imag_shift[n]
        by_real, by_imag = gap / modulus, imag_shift[n] / modulus
        real, imag = far[k, 0, 0], far[k, 0, 1]
        for z in range(1, outer):
            real, imag = real + far[k, z, 0], imag + far[k, z, 1]
        row = pl.multiple_of((plane // cuts) * rows, rows)
        new_real = real * by_real + imag * by_imag
        new_imag = imag * by_real - real * by_imag
        if cuts == 1:
            coarse[k, 0, :, pl.ds(row, rows)] = new_real
            coarse[k, 1, :, pl.ds(row, rows)] = new_imag
        else:
            col = pl.multiple_of(lax.rem(plane, cuts) * cols, cols)
            coarse[k, 0, :, pl.ds(row, rows), pl.ds(col, cols)] = new_real
            coarse[k, 1, :, pl.ds(row, rows), pl.ds(col, cols)] = new_imag
        begin(home_far(k))

    def stage_d(k):
        finish(home_far(k))

        def pick(t, carry):
            for p in range(sep_blocks):
                here = jnp.broadcast_to(maps[t, p, 0:1], (span, wide))
                for c in range(2):
                    value = coarse[k, c, 0]
                    for g in range(1, groups):
                        value = jnp.where(here == float(g), coarse[k, c, g], value)
                    picked[k, t, c, p] = value
            return carry

        lax.fori_loop(0, inner, pick, 0)
        begin(home_near(k))
        own_copy(k, picked.at[k, place], strip(back.at[k], place), 2).start()

    def stage_e(k):
        finish(home_near(k))
        own_copy(k, picked.at[k, place], strip(back.at[k], place), 2).wait()
        n, h = divmod(k, halves)
        right = jnp.concatenate(
            [back[k, c].reshape(sep_blocks * size, wide) for c in range(2)], axis=1
        )
        value = dot_halves((turned_hi[...], turned_lo[...]), split(right))
        value = value.reshape(count, size, 2 * wide)
        for b in range(count):
            chosen = slice(h * wide, (h + 1) * wide)
            lower = jnp.concatenate(
                [whole_residual(b)[:, chosen] - value[b, :, :wide], value[b, :, wide:]], axis=0
            )
            new = dot_halves((fold_hi[n, b], fold_lo[n, b]), split(lower))
            if n > 0:
                new = new + weighted[b, :, chosen]
            weighted[b, :, chosen] = new

    chunks = node_local * halves
    stages = [stage_a, stage_b, stage_c, stage_d, stage_e]
    for k in range(chunks):
        stage_a(k)
    for step in range(1, chunks + len(stages)):
        for s in range(len(stages) - 1, 0, -1):
            k = step - s
            if 0 <= k < chunks:
                stages[s](k)

    part_cols = width // nodes
    for j in range(nodes):
        shares[j] = weighted[:, :, j * part_cols : (j + 1) * part_cols]

    def share_copies(b):
        return [
            remote(
                shares.at[o, b], landed.at[k, b],
                share_send.at[k, b], share_recv.at[k, b], {"node": o},
            )
            for k, o in enumerate(other_nodes)
        ]

    def share_begin(b, carry):
        begin(share_copies(b))
        return carry

    lax.fori_loop(0, count, share_begin, 0)

    def update_step(b, squares):
        finish(share_copies(b))
        total = own_ref[b] - shares[node, b]
        for k in range(nodes - 1):
            total = total - landed[k, b]
        out_ref[b] = total
        return squares + jnp.sum(total * total, axis=0, keepdims=True)

    squares = lax.fori_loop(0, count, update_step, jnp.zeros((1, part_cols), jnp.float32))
    sums[sub] = jnp.broadcast_to(squares, (8, part_cols))
    spread = [
        remote(sums.at[sub], sums.at[sub], sum_send.at[k], sum_recv.at[k], {"sub": o})
        for k, o in enumerate(other_subs)
    ]
    begin(spread)
    finish(spread)
    total = sums[0]
    for t in range(1, subs):
        total = total + sums[t]
    squares_ref[...] = total


def shards(
    search_vectors,
    ritz_values,
    matrix_blocks,
    block_lists,
    inverses,
    panels,
    separator_map,
    separator_shift,
):
    row_count, width = search_vectors.shape
    count, degree, size, _ = matrix_blocks.shape
    nodes, subs = lax.axis_size("node"), lax.axis_size("sub")
    node_local = inverses.shape[0]
    col_count = width // nodes
    sub = lax.axis_index("sub")
    start = lax.axis_index("node") * col_count
    own = lax.dynamic_slice_in_dim(search_vectors, start, col_count, 1)
    own = own.reshape(count, size, col_count)
    own_ritz = lax.dynamic_slice_in_dim(ritz_values, start, col_count, 0)[None, :]
    index = block_lists - sub * count + HALO_BLOCKS

    inner = inner_size(subs)
    outer = subs // inner
    sep_blocks = separator_map.shape[1]
    groups = separator_shift.shape[0] // size
    span = size // inner
    cuts = max(1, outer * 8 // span)
    halves = max(1, width // (size * cuts))
    chunks = node_local * halves
    wide = width // halves
    rows, cols = span * cuts // outer, wide // cuts
    first_row = (sub % inner) * span + (sub // inner // cuts) * rows
    shift = lax.dynamic_slice_in_dim(separator_shift.reshape(groups, size, 1), first_row, rows, 1)
    shift = jnp.broadcast_to(shift, (groups, rows, cols))
    map_tile = jnp.broadcast_to(
        separator_map[0].astype(jnp.float32)[:, None, None], (sep_blocks, 8, wide)
    )
    f32, bf16 = jnp.float32, jnp.bfloat16
    dma = pltpu.SemaphoreType.DMA
    updated, squares = pl.pallas_call(
        functools.partial(kernel, subs, nodes, inner, cuts, halves),
        out_shape=[
            jax.ShapeDtypeStruct(own.shape, f32),
            jax.ShapeDtypeStruct((8, col_count), f32),
        ],
        in_specs=[pl.BlockSpec(memory_space=SMEM)]
        + [pl.BlockSpec(memory_space=VMEM)] * 4
        + [pl.BlockSpec(memory_space=pl.ANY)] * 3,
        out_specs=[pl.BlockSpec(memory_space=VMEM)] * 2,
        scratch_shapes=[
            VMEM(matrix_blocks.shape, f32),
            VMEM(inverses.shape, f32),
            VMEM(panels.shape[1:], f32),
            VMEM((count + 2 * HALO_BLOCKS, size, col_count), f32),
            VMEM((inner, sep_blocks, 8, wide), f32),
            VMEM((nodes, count, size, col_count), f32),
            VMEM(panels.shape[1:], bf16),
            VMEM(panels.shape[1:], bf16),
            VMEM(panels.shape[:0:-1], bf16),
            VMEM(panels.shape[:0:-1], bf16),
            VMEM((node_local, count, size, 2 * size), bf16),
            VMEM((node_local, count, size, 2 * size), bf16),
            VMEM((chunks, count, size, 2 * wide), bf16),
            VMEM((chunks, count, size, 2 * wide), bf16),
            VMEM((chunks, 2, sep_blocks, size, wide), f32),
            VMEM((chunks, inner, 2, sep_blocks, span, wide), f32),
            VMEM((chunks, 2, groups, span, wide), f32),
            VMEM((chunks, outer, 2, groups, rows, cols), f32),
            VMEM((chunks, 2, groups, span, wide), f32),
            VMEM((chunks, inner, 2, sep_blocks, span, wide), f32),
            VMEM((chunks, 2, sep_blocks, size, wide), f32),
            VMEM((count, size, width), f32),
            VMEM((nodes, count, size, col_count), f32),
            VMEM((nodes - 1, count, size, col_count), f32),
            VMEM((subs, 8, col_count), f32),
            dma((5,)),
            dma((2,)),
            dma((2,)),
            dma((inner - 1,)),
            dma((inner - 1,)),
            dma((nodes - 1, count)),
            dma((nodes - 1, count)),
            dma((chunks, 2, inner - 1)),
            dma((chunks, 2, inner - 1)),
            dma((chunks, 2, outer - 1)),
            dma((chunks, 2, outer - 1)),
            dma((chunks, 3)),
            dma((nodes - 1, count)),
            dma((nodes - 1, count)),
            dma((subs - 1,)),
            dma((subs - 1,)),
        ],
        compiler_params=pltpu.CompilerParams(
            collective_id=0, has_side_effects=True, vmem_limit_bytes=60 * 1024 * 1024
        ),
        name="update",
    )(index, map_tile, own, own_ritz, shift, matrix_blocks, inverses, panels[0])
    factor = lax.rsqrt(squares[0:1] / (row_count * subs) + 1e-06)
    return (updated * factor[None]).reshape(row_count, col_count)


def solution(mesh):
    return jax.shard_map(
        shards,
        mesh=mesh,
        in_specs=(
            P("sub", None),
            P(),
            P("sub", None, None, None),
            P("sub", None),
            P("node", None, "sub", None, None),
            P("sub", None, None),
            P("sub", None),
            P(),
        ),
        out_specs=P("sub", "node"),
        check_vma=False,
    )
```

time: 348 us -> 116 us (0.33)
  waiting for transfers between devices: 195 us -> 0 us
  Pallas kernels: 0 us -> 107 us
  matrix products: 45.1 us -> 0 us
  blocking collectives: 41.9 us -> 0 us
  local copies, waits for them, and re-layouts: 27.8 us -> 5.03 us
  between operations: 13.5 us -> 0.01 us
  other arithmetic: 14.9 us -> 3.8 us
  starting transfers between devices: 6.56 us -> 0 us
    psum x1 -> x0, waiting for transfers between devices: 169 us -> none  [shards(): summed_all = lax.psum(spread, 'sub')]
    pallas_call x0 -> x1, Pallas kernels: none -> 107 us  [shards(): pl.pallas_call(functools.partial(kernel, subs, nodes, inner, cuts, halves...]
    dot_general x7 -> x0, matrix products: 45.1 us -> none  [the longest x1 15 us: shards(): jnp.einsum('sr,ncrm->ncsm', my_panel, first_guess, precision=HIGHEST)]
    psum x1 -> x0, blocking collectives: 41.9 us -> none  [shards(): squares = lax.psum(jnp.sum(updated * updated, axis=0), 'sub')]
    ppermute x2 -> x0, waiting for transfers between devices: 9.2 us -> none  [the longest x1 7.18 us: with_halo(): before = lax.ppermute(last, axis, up)]
    all_gather x1 -> x0, waiting for transfers between devices: 8.89 us -> none  [shards(): residual = lax.all_gather(local_part, 'node', axis=1, tiled=True)]
    transpose x4 -> x0, local copies, waits for them, and re-layouts: 8.24 us -> none  [the longest x1 4.17 us: shards(): jnp.einsum('ncbij,ndbjm->ncdbim', inverses, spread_back, precision=HIGHEST)]
    reduce_scatter x1 -> x0, waiting for transfers between devices: 7.57 us -> none  [shards(): lax.psum_scatter(weighted, 'node', scatter_dimension=1, tiled=True)]
  transfers between devices with their start and end apart: 5 -> 0, of which waited for: 5 -> 0; matrix products, arithmetic and copies ran while one was open for 1% -> 0% of each run, Pallas kernels for 0% -> 0%
where the time goes in v2:
time: 116 us; the launch traced here: 115 us
  Pallas kernels  107 us (92%)
  local copies, waits for them, and re-layouts  5.03 us (4%)
  other arithmetic  3.8 us (3%)
    pallas_call x1, Pallas kernels, shards(): pl.pallas_call(functools.partial(kernel, subs, nodes, inner, cuts, halves...  107 us
    mul x2, other arithmetic, shards(): return (updated * factor[None]).reshape(row_count, col_count)  2.55 us

profile of v2, /device:TPU:0, one launch (start us, length us, event | category | flops | bytes accessed | tf_op | source)
XLA Modules:
  0.0 115.4 jit_solution(10172015932091229238)
XLA Ops:
  0.0 0.0 copy-start
  0.0 1.3 %dynamic-slice_bitcast_fusion.1.ritz_ref = f32[1,128]{1,0:T(1,128)} fusion(f32[256]{0:T(256)} %param.9, s32[]{:T(128)S(6)} %select_n.19), kind=kLoop, calls=%fused_computation.4 | loop fusion | bytes 1028 | tf_op jit(solution)/shard_map/broadcast_in_dim | solution.py:422
  1.3 0.7 convert_bitcast_fusion
  2.0 0.8 dynamic-slice_bitcast_fusion
  2.8 0.8 copy.9
  3.5 0.6 subtract_add_fusion.index_ref
  4.1 0.7 broadcast_in_dim.8.map_ref
  4.8 0.7 broadcast_in_dim.20.shift_ref
  5.5 0.0 copy-done
  5.5 0.8 constant_dynamic-slice_fusion
  6.3 106.5 %update.1 = (f32[8,128,128]{2,1,0:T(8,128)}, f32[8,128]{1,0:T(8,128)}) custom-call(s32[8,4]{1,0:T(8,128)} %subtract_add_fusion.index_ref, f32[4,8,128]{2,1,0:T(8,128)} %broadcast_in_dim.8.map_ref, f32[8,128,128]{2,1,0:T(8,128)} %bitcast.13, f32[1,128]{1,0:T(1,128)} %dynamic-slice_bitcast_fusion.1.ritz_ref, f32[8,8,128]{2,1,0:T(8,128)} %broadcast_in_dim.20.shift_ref, ...), custom_call_target="tpu_custom_call" | custom-call | tf_op jit(solution)/shard_map/update/pallas_call | solution.py:443
  112.8 0.7 rsqrt_bitcast_fusion
  113.5 1.9 %broadcast_multiply_fusion = f32[8,128,128]{2,1,0:T(8,128)} fusion(f32[8,128,128]{2,1,0:T(8,128)} %get-tuple-element.7, f32[128]{0:T(128)S(1)} %rsqrt_bitcast_fusion), kind=kLoop, calls=%fused_computation | loop fusion | flops 131072 | bytes 1049088 | tf_op jit(solution)/shard_map/mul | solution.py:502
Async XLA Ops:
  0.0 5.5 %copy-start = (f32[1024,256]{1,0:T(8,128)S(1)}, f32[1024,256]{1,0:T(8,128)}, u32[]{:S(2)}) copy-start(f32[1024,256]{1,0:T(8,128)} %param.8) | copy-start | bytes 3145732

commit v3 on v2

--- a/solution.py
+++ b/solution.py
@@ -55,10 +55,10 @@
 
 
 def kernel(
-    subs, nodes, inner, cuts, halves,
-    index_ref, map_ref, own_ref, ritz_ref, shift_ref, blocks_hbm, inverses_hbm, panel_hbm,
-    out_ref, squares_ref,
-    blocks, inverses, panel, padded, maps, residual,
+    subs, nodes, inner, halves, sliced,
+    index_ref, map_ref, ritz_ref, shift_ref, vectors_hbm, blocks_hbm, inverses_hbm, panel_hbm,
+    out_ref, factor_ref,
+    own_ref, shift_columns, blocks, inverses, panel, padded, maps, residual,
     panel_hi, panel_lo, turned_hi, turned_lo, fold_hi, fold_lo, guess_hi, guess_lo,
     part, near, dense, far, coarse, picked, back, weighted, shares, landed, sums,
     load_sem, halo_send, halo_recv, map_send, map_recv, node_send, node_recv,
@@ -70,15 +70,19 @@
     node_local = inverses.shape[0]
     total_nodes = node_local * nodes
     outer = subs // inner
-    sep_blocks = map_ref.shape[0]
-    groups, rows, cols = shift_ref.shape
+    sep_blocks = map_ref.shape[1]
+    groups = shift_ref.shape[0]
+    rounds = far.shape[1]
     span = size // inner
     wide = part.shape[-1]
     width = wide * halves
     place, plane = lax.rem(sub, inner), sub // inner
     base = plane * inner
     near_places = [lax.rem(place + k, inner) for k in range(1, inner)]
-    far_planes = [lax.rem(plane + k, outer) for k in range(1, outer)]
+    bits = [lax.rem(plane // 2**i, 2) for i in range(rounds)]
+    partners = [
+        {"sub": (plane + 2**i - 2 * 2**i * bits[i]) * inner + place} for i in range(rounds)
+    ]
     other_nodes = [lax.rem(node + k, nodes) for k in range(1, nodes)]
     other_subs = [lax.rem(sub + k, subs) for k in range(1, subs)]
     after, before = lax.rem(sub + 1, subs), lax.rem(sub + subs - 1, subs)
@@ -87,11 +91,30 @@
         pltpu.make_async_copy(panel_hbm, panel, load_sem.at[0]),
         pltpu.make_async_copy(inverses_hbm, inverses, load_sem.at[1]),
         pltpu.make_async_copy(blocks_hbm, blocks, load_sem.at[2]),
-        pltpu.make_async_copy(own_ref, padded.at[pl.ds(HALO_BLOCKS, count)], load_sem.at[3]),
-        pltpu.make_async_copy(map_ref, maps.at[place], load_sem.at[4]),
-    ]
+    ]
+    if sliced:
+        fetch = vectors_hbm
+    else:
+        part_cols = vectors_hbm.shape[2] // nodes
+        first = pl.multiple_of(node * part_cols, part_cols)
+        fetch = vectors_hbm.at[:, :, pl.ds(first, part_cols)]
+    fetch = pltpu.make_async_copy(fetch, own_ref, load_sem.at[3])
+    fetch.start()
     for load in loads:
         load.start()
+    for p in range(sep_blocks):
+        value = map_ref[0, p].astype(jnp.float32)
+        maps[place, p] = jnp.full(maps.shape[2:], value, jnp.float32)
+    ritz_parts = [
+        ritz_ref[:, j * own_ref.shape[2] : (j + 1) * own_ref.shape[2]] for j in range(nodes)
+    ]
+    ritz = ritz_parts[0]
+    for j in range(1, nodes):
+        ritz = jnp.where(node == j, ritz_parts[j], ritz)
+    shift_columns[...] = jnp.concatenate(
+        [shift_ref[...], jnp.zeros((size - groups, size), jnp.float32)], axis=0
+    ).T
+    fetch.wait()
     meet([{"sub": o} for o in other_subs] + [{"node": o} for o in other_nodes])
     halo = [
         remote(
@@ -106,7 +129,7 @@
         ),
     ]
     tell = [
-        remote(map_ref, maps.at[place], map_send.at[k], map_recv.at[k], {"sub": base + t})
+        remote(maps.at[place], maps.at[place], map_send.at[k], map_recv.at[k], {"sub": base + t})
         for k, t in enumerate(near_places)
     ]
     for copy in halo + tell:
@@ -148,8 +171,18 @@
             return carry
 
         lax.fori_loop(0, count, fold, 0)
-    for load in loads[2:]:
-        load.wait()
+    loads[2].wait()
+
+    def diagonal(b, carry):
+        out_ref[b] = dot3(blocks[b, 0], own_ref[b]) - own_ref[b] * ritz
+        return carry
+
+    lax.fori_loop(0, count, diagonal, 0)
+    place_own = pltpu.make_async_copy(
+        own_ref, padded.at[pl.ds(HALO_BLOCKS, count)], load_sem.at[4]
+    )
+    place_own.start()
+    place_own.wait()
     for copy in halo:
         copy.wait()
 
@@ -163,9 +196,11 @@
         ]
 
     def residual_step(b, carry):
-        total = -(own_ref[b] * ritz_ref[...])
-        for q in range(blocks.shape[1]):
-            total = total + dot3(blocks[b, q], padded[index_ref[b, q]])
+        total = out_ref[b]
+        for q in range(1, blocks.shape[1]):
+            spot = index_ref[b, q] - sub * count + HALO_BLOCKS
+            spot = jnp.clip(spot, 0, padded.shape[0] - 1)
+            total = total + dot3(blocks[b, q], padded[spot])
         residual[node, b] = total
         for copy in node_copies(b):
             copy.start()
@@ -176,11 +211,12 @@
     def whole_residual(b):
         return jnp.concatenate([residual[j, b] for j in range(nodes)], axis=1)
 
-    def guess_step(b, carry):
-        for copy in node_copies(b):
-            copy.wait()
-        right = split(whole_residual(b))
-        for n in range(node_local):
+    def guess(n):
+        def step(b, carry):
+            if n == 0:
+                for copy in node_copies(b):
+                    copy.wait()
+            right = split(whole_residual(b))
             for c in range(2):
                 hi, lo = split(dot_halves(split(inverses[n, c, b]), right))
                 for h in range(halves):
@@ -189,21 +225,35 @@
                     spot = slice(c * wide, (c + 1) * wide)
                     guess_hi[k, b, :, spot] = hi[:, chosen]
                     guess_lo[k, b, :, spot] = lo[:, chosen]
-        return carry
-
-    lax.fori_loop(0, count, guess_step, 0)
+            return carry
+
+        lax.fori_loop(0, count, step, 0)
+
     for copy in tell:
         copy.wait()
 
     def strip(ref, t):
         return ref.at[:, :, pl.ds(pl.multiple_of(t * span, span), span)]
 
-    def spot(ref, o):
-        row = pl.multiple_of((o // cuts) * rows, rows)
-        if cuts == 1:
-            return ref.at[:, :, pl.ds(row, rows)]
-        col = pl.multiple_of(lax.rem(o, cuts) * cols, cols)
-        return ref.at[:, :, pl.ds(row, rows), pl.ds(col, cols)]
+    def region(level, other=False):
+        row, col, row_size, col_size = 0, 0, span, wide
+        for i in range(level):
+            bit = 1 - bits[i] if other and i == level - 1 else bits[i]
+            if row_size >= 16:
+                row_size //= 2
+                row = row + bit * row_size
+            else:
+                col_size //= 2
+                col = col + bit * col_size
+        if not isinstance(row, int):
+            row = pl.multiple_of(row, 8)
+        if not isinstance(col, int):
+            col = pl.multiple_of(col, 128)
+        return pl.ds(row, row_size), pl.ds(col, col_size)
+
+    def corner(level):
+        row, col = region(level)
+        return pl.ds(0, row.size), pl.ds(0, col.size)
 
     def own_copy(k, src, dst, which):
         return pltpu.make_async_copy(src, dst, own_sem.at[k, which])
@@ -217,22 +267,22 @@
             for i, t in enumerate(near_places)
         ]
 
-    def there_far(k):
+    def there_far(k, i):
         return [
             remote(
-                spot(dense.at[k], z), far.at[k, plane],
-                far_send.at[k, 0, i], far_recv.at[k, 0, i], {"sub": z * inner + place},
-            )
-            for i, z in enumerate(far_planes)
+                dense.at[(k, slice(None), slice(None)) + region(i + 1, True)],
+                far.at[(k, i, slice(None), slice(None)) + corner(i + 1)],
+                far_send.at[k, 0, i], far_recv.at[k, 0, i], partners[i],
+            )
         ]
 
-    def home_far(k):
+    def home_far(k, i):
+        mine = (k, slice(None), slice(None)) + region(i + 1)
         return [
             remote(
-                spot(coarse.at[k], plane), spot(coarse.at[k], plane),
-                far_send.at[k, 1, i], far_recv.at[k, 1, i], {"sub": z * inner + place},
-            )
-            for i, z in enumerate(far_planes)
+                coarse.at[mine], coarse.at[mine],
+                far_send.at[k, 1, i], far_recv.at[k, 1, i], partners[i],
+            )
         ]
 
     def home_near(k):
@@ -288,33 +338,37 @@
             return carry
 
         lax.fori_loop(0, groups, group, 0)
-        begin(there_far(k))
-        own_copy(k, spot(dense.at[k], plane), far.at[k, plane], 1).start()
-
-    def stage_c(k):
-        finish(there_far(k))
-        own_copy(k, spot(dense.at[k], plane), far.at[k, plane], 1).wait()
+        begin(there_far(k, 0))
+
+    def stage_c(k, i):
+        finish(there_far(k, i))
+        mine = (k, slice(None), slice(None)) + region(i + 1)
+        value = dense[mine] + far[(k, i, slice(None), slice(None)) + corner(i + 1)]
+        if i < rounds - 1:
+            dense[mine] = value
+            begin(there_far(k, i + 1))
+            return
         n = k // halves
-        gap = real_shift[n] - shift_ref[...]
-        modulus = gap * gap + imag_shift[n] * imag_shift[n]
-        by_real, by_imag = gap / modulus, imag_shift[n] / modulus
-        real, imag = far[k, 0, 0], far[k, 0, 1]
-        for z in range(1, outer):
-            real, imag = real + far[k, z, 0], imag + far[k, z, 1]
-        row = pl.multiple_of((plane // cuts) * rows, rows)
-        new_real = real * by_real + imag * by_imag
-        new_imag = imag * by_real - real * by_imag
-        if cuts == 1:
-            coarse[k, 0, :, pl.ds(row, rows)] = new_real
-            coarse[k, 1, :, pl.ds(row, rows)] = new_imag
-        else:
-            col = pl.multiple_of(lax.rem(plane, cuts) * cols, cols)
-            coarse[k, 0, :, pl.ds(row, rows), pl.ds(col, cols)] = new_real
-            coarse[k, 1, :, pl.ds(row, rows), pl.ds(col, cols)] = new_imag
-        begin(home_far(k))
+        row, col = region(rounds)
+        first = pl.multiple_of(place * span + row.start, 8)
+        columns = shift_columns[pl.ds(first, row.size)]
+        for g in range(groups):
+            gap = real_shift[n] - columns[:, g : g + 1]
+            modulus = gap * gap + imag_shift[n] * imag_shift[n]
+            shape = (row.size, col.size)
+            by_real = jnp.broadcast_to(gap / modulus, shape)
+            by_imag = jnp.broadcast_to(imag_shift[n] / modulus, shape)
+            real, imag = value[0, g], value[1, g]
+            coarse[k, 0, g, row, col] = real * by_real + imag * by_imag
+            coarse[k, 1, g, row, col] = imag * by_real - real * by_imag
+        begin(home_far(k, rounds - 1))
+
+    def stage_h(k, i):
+        finish(home_far(k, i))
+        begin(home_far(k, i - 1))
 
     def stage_d(k):
-        finish(home_far(k))
+        finish(home_far(k, 0))
 
         def pick(t, carry):
             for p in range(sep_blocks):
@@ -350,14 +404,18 @@
             weighted[b, :, chosen] = new
 
     chunks = node_local * halves
-    stages = [stage_a, stage_b, stage_c, stage_d, stage_e]
-    for k in range(chunks):
-        stage_a(k)
-    for step in range(1, chunks + len(stages)):
-        for s in range(len(stages) - 1, 0, -1):
-            k = step - s
-            if 0 <= k < chunks:
-                stages[s](k)
+    stages = [stage_b]
+    stages += [functools.partial(stage_c, i=i) for i in range(rounds)]
+    stages += [functools.partial(stage_h, i=i) for i in range(rounds - 1, 0, -1)]
+    stages += [stage_d, stage_e]
+    for n in range(node_local):
+        guess(n)
+        for h in range(halves):
+            stage_a(n * halves + h)
+    for step in range(chunks + len(stages) - 1):
+        for s, stage in enumerate(stages):
+            if 0 <= step - s < chunks:
+                stage(step - s)
 
     part_cols = width // nodes
     for j in range(nodes):
@@ -397,7 +455,8 @@
     total = sums[0]
     for t in range(1, subs):
         total = total + sums[t]
-    squares_ref[...] = total
+    rows = count * size * subs
+    factor_ref[...] = lax.rsqrt(total / rows + 1e-06)
 
 
 def shards(
@@ -415,42 +474,37 @@
     nodes, subs = lax.axis_size("node"), lax.axis_size("sub")
     node_local = inverses.shape[0]
     col_count = width // nodes
-    sub = lax.axis_index("sub")
-    start = lax.axis_index("node") * col_count
-    own = lax.dynamic_slice_in_dim(search_vectors, start, col_count, 1)
-    own = own.reshape(count, size, col_count)
-    own_ritz = lax.dynamic_slice_in_dim(ritz_values, start, col_count, 0)[None, :]
-    index = block_lists - sub * count + HALO_BLOCKS
+    vectors = search_vectors
+    sliced = col_count % 128 != 0
+    if sliced:
+        start = lax.axis_index("node") * col_count
+        vectors = lax.dynamic_slice_in_dim(vectors, start, col_count, 1)
+    vectors = vectors.reshape(count, size, -1)
 
     inner = inner_size(subs)
     outer = subs // inner
     sep_blocks = separator_map.shape[1]
     groups = separator_shift.shape[0] // size
     span = size // inner
-    cuts = max(1, outer * 8 // span)
-    halves = max(1, width // (size * cuts))
+    rounds = max(1, (outer - 1).bit_length())
+    halves = width // size if span // outer >= 8 else 1
     chunks = node_local * halves
     wide = width // halves
-    rows, cols = span * cuts // outer, wide // cuts
-    first_row = (sub % inner) * span + (sub // inner // cuts) * rows
-    shift = lax.dynamic_slice_in_dim(separator_shift.reshape(groups, size, 1), first_row, rows, 1)
-    shift = jnp.broadcast_to(shift, (groups, rows, cols))
-    map_tile = jnp.broadcast_to(
-        separator_map[0].astype(jnp.float32)[:, None, None], (sep_blocks, 8, wide)
-    )
     f32, bf16 = jnp.float32, jnp.bfloat16
     dma = pltpu.SemaphoreType.DMA
-    updated, squares = pl.pallas_call(
-        functools.partial(kernel, subs, nodes, inner, cuts, halves),
+    updated, factor = pl.pallas_call(
+        functools.partial(kernel, subs, nodes, inner, halves, sliced),
         out_shape=[
-            jax.ShapeDtypeStruct(own.shape, f32),
+            jax.ShapeDtypeStruct((count, size, col_count), f32),
             jax.ShapeDtypeStruct((8, col_count), f32),
         ],
-        in_specs=[pl.BlockSpec(memory_space=SMEM)]
-        + [pl.BlockSpec(memory_space=VMEM)] * 4
-        + [pl.BlockSpec(memory_space=pl.ANY)] * 3,
+        in_specs=[pl.BlockSpec(memory_space=SMEM)] * 2
+        + [pl.BlockSpec(memory_space=VMEM)] * 2
+        + [pl.BlockSpec(memory_space=pl.ANY)] * 4,
         out_specs=[pl.BlockSpec(memory_space=VMEM)] * 2,
         scratch_shapes=[
+            VMEM((count, size, col_count), f32),
+            VMEM((size, size), f32),
             VMEM(matrix_blocks.shape, f32),
             VMEM(inverses.shape, f32),
             VMEM(panels.shape[1:], f32),
@@ -468,7 +522,7 @@
             VMEM((chunks, 2, sep_blocks, size, wide), f32),
             VMEM((chunks, inner, 2, sep_blocks, span, wide), f32),
             VMEM((chunks, 2, groups, span, wide), f32),
-            VMEM((chunks, outer, 2, groups, rows, cols), f32),
+            VMEM((chunks, rounds, 2, groups, span // 2, wide), f32),
             VMEM((chunks, 2, groups, span, wide), f32),
             VMEM((chunks, inner, 2, sep_blocks, span, wide), f32),
             VMEM((chunks, 2, sep_blocks, size, wide), f32),
@@ -485,8 +539,8 @@
             dma((nodes - 1, count)),
             dma((chunks, 2, inner - 1)),
             dma((chunks, 2, inner - 1)),
-            dma((chunks, 2, outer - 1)),
-            dma((chunks, 2, outer - 1)),
+            dma((chunks, 2, rounds)),
+            dma((chunks, 2, rounds)),
             dma((chunks, 3)),
             dma((nodes - 1, count)),
             dma((nodes - 1, count)),
@@ -497,9 +551,11 @@
             collective_id=0, has_side_effects=True, vmem_limit_bytes=60 * 1024 * 1024
         ),
         name="update",
-    )(index, map_tile, own, own_ritz, shift, matrix_blocks, inverses, panels[0])
-    factor = lax.rsqrt(squares[0:1] / (row_count * subs) + 1e-06)
-    return (updated * factor[None]).reshape(row_count, col_count)
+    )(
+        block_lists, separator_map, ritz_values[None], separator_shift.reshape(groups, size),
+        vectors, matrix_blocks, inverses, panels[0],
+    )
+    return (updated * factor[None, 0:1]).reshape(row_count, col_count)
 
 
 def solution(mesh):

time: 116 us -> 102 us (0.88)
  Pallas kernels: 107 us -> 98.2 us
  local copies, waits for them, and re-layouts: 5.03 us -> 2.02 us
  other arithmetic: 3.8 us -> 1.87 us
    pallas_call x1, Pallas kernels: 107 us -> 98.2 us  [shards(): pl.pallas_call(functools.partial(kernel, subs, nodes, inner, halves, slic...]
    broadcast_in_dim x4 -> x0, local copies, waits for them, and re-layouts: 3.44 us -> none  [the longest x2 1.44 us: shards(): shift = jnp.broadcast_to(shift, (groups, rows, cols))]
    mul x2 -> x1, other arithmetic: 2.55 us -> 1.87 us  [shards(): return (updated * factor[None, 0:1]).reshape(row_count, col_count)]
where the time goes in v3:
time: 102 us
  Pallas kernels  98.2 us (96%)
  local copies, waits for them, and re-layouts  2.02 us (2%)
  other arithmetic  1.87 us (2%)
    pallas_call x1, Pallas kernels, shards(): pl.pallas_call(functools.partial(kernel, subs, nodes, inner, halves, slic...  98.2 us

profile of v3, /device:TPU:0, one launch (start us, length us, event | category | flops | bytes accessed | tf_op | source)
XLA Modules:
  0.0 102.1 jit_solution(18316781326849676166)
XLA Ops:
  0.0 1.3 %copy.9.index_ref = s32[8,4]{1,0:T(8,128)} copy(s32[8,4]{0,1:T(4,128)} %param.11) | data formatting | bytes 256 | tf_op args[3]
  1.3 98.2 %update.1 = (f32[8,128,128]{2,1,0:T(8,128)}, f32[8,128]{1,0:T(8,128)}) custom-call(s32[8,4]{1,0:T(8,128)} %copy.9.index_ref, s32[1,4]{1,0:T(1,128)} %map_ref.1, f32[1,256]{1,0:T(1,128)} %bitcast.10, f32[8,128]{1,0:T(8,128)} %bitcast.9, f32[8,128,256]{2,1,0:T(8,128)} %bitcast.8, f32[8,4,128,128]{3,2,1,0:T(8,128)} %blocks_hbm.1, ...), custom_call_target="tpu_custom_call" | custom-call | tf_op jit(solution)/shard_map/update/pallas_call | solution.py:495
  99.6 0.7 slice_bitcast_fusion
  100.3 1.9 %broadcast_multiply_fusion = f32[8,128,128]{2,1,0:T(8,128)} fusion(f32[8,128,128]{2,1,0:T(8,128)} %get-tuple-element.7, f32[128]{0:T(128)S(1)} %slice_bitcast_fusion), kind=kLoop, calls=%fused_computation | loop fusion | flops 131072 | bytes 1049088 | tf_op jit(solution)/shard_map/mul | solution.py:558

commit v4 on v3

--- a/solution.py
+++ b/solution.py
@@ -156,9 +156,6 @@
         hi, lo = split(block)
         panel_hi[p * size : (p + 1) * size] = hi
         panel_lo[p * size : (p + 1) * size] = lo
-        hi, lo = split(block.T)
-        turned_hi[:, p * size : (p + 1) * size] = hi
-        turned_lo[:, p * size : (p + 1) * size] = lo
     loads[1].wait()
     for n in range(node_local):
 
@@ -403,6 +400,11 @@
                 new = new + weighted[b, :, chosen]
             weighted[b, :, chosen] = new
 
+    def turn(p):
+        hi, lo = split(panel[p * size : (p + 1) * size].T)
+        turned_hi[:, p * size : (p + 1) * size] = hi
+        turned_lo[:, p * size : (p + 1) * size] = lo
+
     chunks = node_local * halves
     stages = [stage_b]
     stages += [functools.partial(stage_c, i=i) for i in range(rounds)]
@@ -416,6 +418,9 @@
         for s, stage in enumerate(stages):
             if 0 <= step - s < chunks:
                 stage(step - s)
+        for p in range(sep_blocks):
+            if p % (len(stages) - 2) == step:
+                turn(p)
 
     part_cols = width // nodes
     for j in range(nodes):
@@ -456,7 +461,7 @@
     for t in range(1, subs):
         total = total + sums[t]
     rows = count * size * subs
-    factor_ref[...] = lax.rsqrt(total / rows + 1e-06)
+    factor_ref[...] = lax.rsqrt(total[0:1] / rows + 1e-06)
 
 
 def shards(
@@ -496,7 +501,7 @@
         functools.partial(kernel, subs, nodes, inner, halves, sliced),
         out_shape=[
             jax.ShapeDtypeStruct((count, size, col_count), f32),
-            jax.ShapeDtypeStruct((8, col_count), f32),
+            jax.ShapeDtypeStruct((1, col_count), f32),
         ],
         in_specs=[pl.BlockSpec(memory_space=SMEM)] * 2
         + [pl.BlockSpec(memory_space=VMEM)] * 2
@@ -555,7 +560,7 @@
         block_lists, separator_map, ritz_values[None], separator_shift.reshape(groups, size),
         vectors, matrix_blocks, inverses, panels[0],
     )
-    return (updated * factor[None, 0:1]).reshape(row_count, col_count)
+    return (updated * factor[None]).reshape(row_count, col_count)
 
 
 def solution(mesh):

time: 102 us -> 102 us (level)
  no operation moved by 1% of the time
where the time goes in v4:
time: 102 us; the launch traced here: 101 us
  Pallas kernels  98.2 us (96%)
  other arithmetic  1.87 us (2%)
  local copies, waits for them, and re-layouts  1.35 us (1%)
    pallas_call x1, Pallas kernels, shards(): pl.pallas_call(functools.partial(kernel, subs, nodes, inner, halves, slic...  98.2 us

profile of v4, /device:TPU:0, one launch (start us, length us, event | category | flops | bytes accessed | tf_op | source)
XLA Modules:
  0.0 101.5 jit_solution(1502563342728047730)
XLA Ops:
  0.0 1.3 %copy.9.index_ref = s32[8,4]{1,0:T(8,128)} copy(s32[8,4]{0,1:T(4,128)} %param.11) | data formatting | bytes 256 | tf_op args[3]
  1.3 98.2 %update.1 = (f32[8,128,128]{2,1,0:T(8,128)}, f32[1,128]{1,0:T(1,128)}) custom-call(s32[8,4]{1,0:T(8,128)} %copy.9.index_ref, s32[1,4]{1,0:T(1,128)} %map_ref.1, f32[1,256]{1,0:T(1,128)} %bitcast.9, f32[8,128]{1,0:T(8,128)} %bitcast.8, f32[8,128,256]{2,1,0:T(8,128)} %bitcast.7, f32[8,4,128,128]{3,2,1,0:T(8,128)} %blocks_hbm.1, ...), custom_call_target="tpu_custom_call" | custom-call | tf_op jit(solution)/shard_map/update/pallas_call | solution.py:500
  99.6 1.9 %broadcast_multiply_fusion = f32[8,128,128]{2,1,0:T(8,128)} fusion(f32[8,128,128]{2,1,0:T(8,128)} %get-tuple-element.7, f32[128]{0:T(128)} %bitcast.10), kind=kLoop, calls=%fused_computation | loop fusion | flops 131072 | bytes 1049088 | tf_op jit(solution)/shard_map/mul | solution.py:563

commit v5 on v4

--- a/solution.py
+++ b/solution.py
@@ -111,11 +111,8 @@
     ritz = ritz_parts[0]
     for j in range(1, nodes):
         ritz = jnp.where(node == j, ritz_parts[j], ritz)
-    shift_columns[...] = jnp.concatenate(
-        [shift_ref[...], jnp.zeros((size - groups, size), jnp.float32)], axis=0
-    ).T
+    meet([{"sub": o} for o in other_subs] + [{"node": o} for o in other_nodes])
     fetch.wait()
-    meet([{"sub": o} for o in other_subs] + [{"node": o} for o in other_nodes])
     halo = [
         remote(
             own_ref.at[pl.ds(count - HALO_BLOCKS, HALO_BLOCKS)],
@@ -134,6 +131,9 @@
     ]
     for copy in halo + tell:
         copy.start()
+    shift_columns[...] = jnp.concatenate(
+        [shift_ref[...], jnp.zeros((size - groups, size), jnp.float32)], axis=0
+    ).T
 
     def constant(values):
         chosen = jnp.float32(values[0])

time: 102 us -> 102 us (level)
  no operation moved by 1% of the time
where the time goes in v5:
time: 102 us; the launch traced here: 101 us
  Pallas kernels  98.2 us (96%)
  other arithmetic  1.87 us (2%)
  local copies, waits for them, and re-layouts  1.35 us (1%)
    pallas_call x1, Pallas kernels, shards(): pl.pallas_call(functools.partial(kernel, subs, nodes, inner, halves, slic...  98.2 us

profile of v5, /device:TPU:0, one launch (start us, length us, event | category | flops | bytes accessed | tf_op | source)
XLA Modules:
  0.0 101.4 jit_solution(13717007245164236007)
XLA Ops:
  0.0 1.3 %copy.9.index_ref = s32[8,4]{1,0:T(8,128)} copy(s32[8,4]{0,1:T(4,128)} %param.11) | data formatting | bytes 256 | tf_op args[3]
  1.3 98.2 %update.1 = (f32[8,128,128]{2,1,0:T(8,128)}, f32[1,128]{1,0:T(1,128)}) custom-call(s32[8,4]{1,0:T(8,128)} %copy.9.index_ref, s32[1,4]{1,0:T(1,128)} %map_ref.1, f32[1,256]{1,0:T(1,128)} %bitcast.9, f32[8,128]{1,0:T(8,128)} %bitcast.8, f32[8,128,256]{2,1,0:T(8,128)} %bitcast.7, f32[8,4,128,128]{3,2,1,0:T(8,128)} %blocks_hbm.1, ...), custom_call_target="tpu_custom_call" | custom-call | tf_op jit(solution)/shard_map/update/pallas_call | solution.py:500
  99.6 1.9 %broadcast_multiply_fusion = f32[8,128,128]{2,1,0:T(8,128)} fusion(f32[8,128,128]{2,1,0:T(8,128)} %get-tuple-element.7, f32[128]{0:T(128)} %bitcast.10), kind=kLoop, calls=%fused_computation | loop fusion | flops 131072 | bytes 1049088 | tf_op jit(solution)/shard_map/mul | solution.py:563
